TPU v7x, 768 devices: a whole 4x8x12 slice. The times are simulated.
768 devices in a mesh: dp: 24 (over z_lo, x), vocab: 32 (over y, z_hi, core).
Axes of the slice: x: 4, y: 8, z: 12 (z_hi: 2, z_lo: 6; z = z_hi * 6 + z_lo), core: 2. Of those that a mesh axis runs over, the one named last changes fastest.
Arguments:
- hidden: bfloat16 [768, 4608], P('dp'), may hold values from -18 to 18
- weight: bfloat16 [4608, 76032], P('dp', 'vocab'), may hold values from -1 to 1
- targets: int32 [768], replicated, may hold values from 0 to 76031
- advantage: float32 [768], replicated, may hold values from -4 to 4
- counts: int32 [192], replicated, may hold values from 0 to 4
- block_order: int32 [192], replicated, may hold values from 0 to 191, each once
Outputs:
- logprob: float32 [768], P('dp')
- hidden_grad: bfloat16 [768, 4608], P('vocab', 'dp')
All inputs are finite; a program needn't handle non-finite values.
Results may differ from a plain program's by a relative error of at most 0.0049.
Values may be sent and summed in bfloat16 or wider, within the bound.
No kernel may reach another device: no remote copies, remote signals or barrier semaphores. Data moves between devices by JAX's collectives and lax.ppermute only.
A program may use at most 32 MiB of HBM per device.

v0:
```python
import jax
import jax.numpy as jnp
from jax import lax
from jax.sharding import PartitionSpec as P

BLK = 4


def merged(part, axis, combine):
    gathered = jax.tree.map(lambda a: lax.all_gather(a, axis), part)

    def take(source):
        return jax.tree.map(lambda a: lax.dynamic_index_in_dim(a, source, 0, False), gathered)

    return lax.fori_loop(
        1, lax.axis_size(axis), lambda source, state: combine(state, take(source)), take(0)
    )


def combine(first, second):
    top = jnp.maximum(first[0], second[0])
    total = first[1] * jnp.exp(first[0] - top) + second[1] * jnp.exp(second[0] - top)
    return (top, total, first[2] + second[2])


def local_stats(logits, wanted, columns):
    hit = wanted[:, None] == columns[None, :]
    top = jnp.max(logits, axis=1)
    total = jnp.sum(jnp.exp(logits - top[:, None]), axis=1)
    target_logit = jnp.sum(jnp.where(hit, logits, jnp.float32(0.0)), axis=1)
    return ((top, total, target_logit), hit)


def logit_grads(logits, lse, hit, coef):
    probs = jnp.exp(logits - lse[:, None])
    return (coef[:, None] * (probs - hit.astype(jnp.float32))).astype(jnp.bfloat16)


def body(hidden, weight, targets, advantage, counts, block_order):
    rows_all = lax.all_to_all(hidden, "dp", split_axis=1, concat_axis=0, tiled=True)
    total_rows = rows_all.shape[0]
    width = weight.shape[1]
    learners = lax.axis_size("dp")
    per_group = total_rows // learners
    position = jnp.arange(total_rows, dtype=jnp.int32)
    blocks = block_order[position // BLK]
    source = blocks * BLK + position % BLK
    ordered = jnp.take(rows_all, source, axis=0)
    wanted_all = targets[source]
    alive = position % BLK < counts[blocks]
    coef_all = jnp.where(alive, advantage[source], jnp.float32(0.0))
    vocab_base = lax.axis_index("vocab") * width
    first_row = lax.axis_index("dp") * per_group
    piece = ordered
    logits = lax.psum_scatter(
        jnp.dot(piece, weight, preferred_element_type=jnp.float32),
        "dp",
        scatter_dimension=0,
        tiled=True,
    )
    wanted = lax.dynamic_slice_in_dim(wanted_all, first_row, per_group, 0)
    coef = lax.dynamic_slice_in_dim(coef_all, first_row, per_group, 0)
    columns = vocab_base + jnp.arange(width, dtype=jnp.int32)
    stats, hit = local_stats(logits, wanted, columns)
    top, summed, target_logit = merged(stats, "vocab", combine)
    lse = top + jnp.log(summed)
    logprob = target_logit - lse
    grads = logit_grads(logits, lse, hit, coef)
    grad_all = lax.all_gather(grads, "dp", axis=0, tiled=True)
    piece = grad_all
    hidden_grad = lax.psum_scatter(
        lax.dot_general(
            piece, weight, (((1,), (1,)), ((), ())), preferred_element_type=jnp.float32
        ),
        "vocab",
        scatter_dimension=0,
        tiled=True,
    )
    return (logprob, hidden_grad.astype(jnp.bfloat16))


def solution(mesh):
    placed = (P("dp", None), P("dp", "vocab"), P(), P(), P(), P())
    return jax.shard_map(
        body, mesh=mesh, in_specs=placed, out_specs=(P("dp"), P("vocab", "dp")), check_vma=False
    )
```

profile of v0, /device:TPU:2, one launch (start us, length us, event | category | flops | bytes accessed | tf_op | source)
XLA Modules:
  0.0 746.1 jit_solution(6441040079285374363)
XLA Ops:
  7.2 0.0 copy-start
  7.2 0.0 copy-start.1
  7.2 1.4 all_to_all.14
  8.6 0.8 copy.9
  9.4 15.2 %all-to-all-start = ((bf16[32,24,192]{2,0,1:T(8,128)(2,1)}), bf16[32,24,192]{2,0,1:T(8,128)(2,1)S(1)}, u32[]{:S(2)}, u32[]{:S(2)}) async-start(bf16[32,24,192]{2,0,1:T(8,128)(2,1)} %copy.9), calls=%async_computation | async-start | bytes 786432 | tf_op jit(solution)/shard_map/all_to_all | solution.py:40
  24.6 0.0 reduce-scatter.3.cloned.1.call-start
  24.7 0.0 copy-done.1
  24.7 5.0 gather_fusion
  29.7 10.9 %all-to-all-done = bf16[32,24,192]{2,0,1:T(8,128)(2,1)S(1)} async-done(((bf16[32,24,192]{2,0,1:T(8,128)(2,1)}), bf16[32,24,192]{2,0,1:T(8,128)(2,1)S(1)}, u32[]{:S(2)}, u32[]{:S(2)}) %all-to-all-start) | async-done | bytes 294944 | tf_op jit(solution)/shard_map/all_to_all | solution.py:40
  40.6 2.6 gather_fusion.1
  43.2 0.0 copy-done
  43.3 4.2 fusion.7
  47.5 0.0 copy-start.3
  47.5 0.0 reduce-scatter.3.cloned.1.call-update
  47.5 0.0 copy-start.4
  47.5 0.0 all-gather.5.cloned.1.call-start
  47.6 0.6 copy-done.3
  48.2 0.0 copy-start.2
  48.2 3.2 gather_fusion.2
  51.4 0.0 copy-done.4
  51.4 3.2 gather_fusion.4
  54.6 0.1 dynamic_slice.48
  54.7 0.0 copy-done.2
  54.7 5.0 gather_fusion.3
  59.7 0.1 dynamic_slice.50
  59.7 1.3 dynamic-slice
  61.7 162.2 %reduce-scatter.3.cloned.1.call-done = f32[32,2376]{1,0:T(8,128)} async-done(((f32[768,2376]{1,0:T(8,128)}), f32[32,2376]{1,0:T(8,128)}) %reduce-scatter.3.cloned.1.call-update) | async-done | bytes 304144 | tf_op jit(solution)/shard_map/reduce_scatter | solution.py:55
  223.9 1.1 reduce_max.9
  225.0 0.2 dynamic-update-slice
  225.3 1.2 fusion.10
  226.5 0.2 dynamic-update-slice.2
  226.8 0.2 dynamic-update-slice.1
  227.0 205.6 %all-reduce.3 = (f32[1024]{0:T(1024)S(1)}, f32[1024]{0:T(1024)S(1)}, f32[1024]{0:T(1024)S(1)}) all-reduce(f32[1024]{0:T(1024)S(1)} %dynamic-update-slice, f32[1024]{0:T(1024)S(1)} %dynamic-update-slice.1, f32[1024]{0:T(1024)S(1)} %dynamic-update-slice.2), channel_id=2, replica_groups=mesh['dp'=24,'vocab'=32] {'vocab'}, use_global_device_ids=true, to_apply=%add | all-reduce | flops 3072 | bytes 24576
  432.6 0.1 reshape.152
  432.7 0.1 reshape.153
  432.7 0.1 reshape.154
  432.8 1.4 while.19
  434.3 0.5 fusion.26
  434.8 1.8 fusion.13
  436.6 0.0 all-gather.5.cloned.1.call-update
  436.6 0.0 reduce-scatter.5.cloned.1.call-start
  436.6 153.9 %all-gather.5.cloned.1.call-done = bf16[768,2376]{1,0:T(8,128)(2,1)} async-done(((bf16[32,2376]{1,0:T(8,128)(2,1)}), bf16[768,2376]{1,0:T(8,128)(2,1)}) %all-gather.5.cloned.1.call-update) | async-done | bytes 3649552 | tf_op jit(solution)/shard_map/all_gather | solution.py:69
  590.6 4.1 fusion.27
  594.7 0.0 reduce-scatter.5.cloned.1.call-update
  594.7 143.5 %reduce-scatter.5.cloned.1.call-done = f32[24,192]{1,0:T(8,128)} async-done(((f32[768,192]{1,0:T(8,128)}), f32[24,192]{1,0:T(8,128)}) %reduce-scatter.5.cloned.1.call-update) | async-done | bytes 18448 | tf_op jit(solution)/shard_map/reduce_scatter | solution.py:71
  738.2 1.3 convert_element_type.11
  (45 shorter events, 1.0 us)
Async XLA Ops:
  7.2 36.1 %copy-start = (bf16[192,2376]{1,0:T(8,128)(2,1)S(1)}, bf16[192,2376]{1,0:T(8,128)(2,1)}, u32[]{:S(2)}) copy-start(bf16[192,2376]{1,0:T(8,128)(2,1)} %param.9) | copy-start | bytes 2737156
  7.2 17.5 %copy-start.1 = (s32[192]{0:T(256)S(1)}, s32[192]{0:T(256)}, u32[]{:S(2)}) copy-start(s32[192]{0:T(256)} %param.13) | copy-start | bytes 2308
  9.4 31.2 %all-to-all-start = ((bf16[32,24,192]{2,0,1:T(8,128)(2,1)}), bf16[32,24,192]{2,0,1:T(8,128)(2,1)S(1)}, u32[]{:S(2)}, u32[]{:S(2)}) async-start(bf16[32,24,192]{2,0,1:T(8,128)(2,1)} %copy.9), calls=%async_computation | async-start | bytes 786432 | tf_op jit(solution)/shard_map/all_to_all | solution.py:40
  24.6 199.3 %reduce-scatter.3.cloned.1.call-start = ((), (), s32[]{:S(2)}) async-start(), calls=%async_computation.3 | async-start | bytes 7782400 | tf_op jit(solution)/shard_map/reduce_scatter | solution.py:55
  47.5 0.7 copy-start.3
  47.5 3.9 copy-start.4
  47.5 543.0 %all-gather.5.cloned.1.call-start = ((), (), s32[]{:S(2)}) async-start(), calls=%async_computation.4 | async-start | bytes 3891200 | tf_op jit(solution)/shard_map/all_gather | solution.py:69
  48.2 6.5 copy-start.2
  436.6 301.6 %reduce-scatter.5.cloned.1.call-start = ((), (), s32[]{:S(2)}) async-start(), calls=%async_computation.5 | async-start | bytes 811008 | tf_op jit(solution)/shard_map/reduce_scatter | solution.py:71
Sparse Core Ops, SparseCore 0:
  47.6 176.2 reduce-scatter.2
  436.7 153.7 all-gather.4
  595.7 142.4 reduce-scatter.4
where the time goes:
time: 747 us; the launch traced here: 746 us
  waiting for transfers between devices  471 us (63%)
  blocking collectives  206 us (28%)
  local copies, waits for them, and re-layouts  24.1 us (3%)
  starting transfers between devices  15.3 us (2%)
  between operations  14.6 us (2%)
  matrix products  8.36 us (1%)
    unnamed x1, blocking collectives  206 us
    reduce_scatter x1, waiting for transfers between devices, body(): lax.psum_scatter(jnp.dot(piece, weight, preferred_element_type=jnp.float3...  162 us
    all_gather x1, waiting for transfers between devices, body(): grad_all = lax.all_gather(grads, 'dp', axis=0, tiled=True)  154 us
    reduce_scatter x1, waiting for transfers between devices, body(): lax.psum_scatter(lax.dot_general(piece, weight, (((1,), (1,)), ((), ())),...  143 us
    all_to_all x1, starting transfers between devices, body(): lax.all_to_all(hidden, 'dp', split_axis=1, concat_axis=0, tiled=True)  15.2 us
  transfers between devices with their start and end apart: 4, of which 4 were waited for; matrix products, arithmetic and copies ran while one was open for 2% of the time, Pallas kernels for 0%

commit v1 on v0

v1 whole, which is shorter than its diff:
```python
import jax
import jax.numpy as jnp
from jax import lax
from jax.sharding import Mesh, PartitionSpec as P

BLK = 4
NZ, NX, NY, NH, NC = 6, 4, 8, 2, 2
VOC = ("y", "zh", "c")
NV = NY * NH * NC
F32, BF16 = jnp.float32, jnp.bfloat16


def roll_to(a, axis, start):
    return lax.dynamic_slice_in_dim(jnp.concatenate([a, a], axis), start, a.shape[axis], axis)


def split3(a):
    hi = lax.reduce_precision(a, 8, 7)
    rest = a - hi
    mid = lax.reduce_precision(rest, 8, 7)
    return jnp.stack([hi, mid, rest - mid], axis=1).astype(BF16)


def join3(cols):
    cols = cols.astype(F32)
    return (cols[:, 0] + cols[:, 1]) + cols[:, 2]


def line_scatter(part):
    right = left = None
    for s in range(1, NZ):
        to_right = part[NZ - s] if right is None else part[NZ - s] + right
        to_left = part[s] if left is None else part[s] + left
        right = lax.ppermute(to_right, "zl", [(i, i + 1) for i in range(s)])
        left = lax.ppermute(to_left, "zl", [(i, i - 1) for i in range(NZ - s, NZ)])
    return part[0] + right + left


def line_gather(block):
    right, left = [block], [block]
    for s in range(1, NZ):
        right.append(lax.ppermute(right[-1], "zl", [(i, i + 1) for i in range(s - 1, NZ - 1)]))
        left.append(lax.ppermute(left[-1], "zl", [(i, i - 1) for i in range(1, NZ - s + 1)]))
    z = lax.axis_index("zl")
    return [block] + [jnp.where(z >= q, right[q], left[NZ - q]) for q in range(1, NZ)]


def body(hidden, weight, targets, advantage, counts, block_order):
    per, model = hidden.shape
    feats, width = weight.shape
    rows = targets.shape[0]
    z, x = lax.axis_index("zl"), lax.axis_index("x")
    v = lax.axis_index(VOC)
    back = [(i, (i - 1) % NX) for i in range(NX)]
    forth = [(i, (i + 1) % NX) for i in range(NX)]

    half = feats // 2
    w1 = lax.ppermute(weight, "x", back)
    w3 = lax.ppermute(weight, "x", forth)
    w2 = jnp.concatenate(
        [lax.ppermute(w1[:half], "x", back), lax.ppermute(w3[half:], "x", forth)], 0
    )
    w = [weight, w1, w2, w3]

    h = hidden.reshape(per, NZ, NX, feats).transpose(1, 2, 0, 3)
    h = lax.all_to_all(h, "zl", split_axis=0, concat_axis=0, tiled=True)
    h = roll_to(roll_to(h, 1, x), 0, z)

    position = jnp.arange(rows, dtype=jnp.int32)
    blocks = block_order[position // BLK]
    source = blocks * BLK + position % BLK
    wanted = targets[source]
    alive = position % BLK < counts[blocks]
    coef = jnp.where(alive, advantage[source], F32(0.0))

    columns = v * width + jnp.arange(width, dtype=jnp.int32)
    onehot = (wanted[:, None] == columns[None, :]).astype(BF16)
    picked = lax.dot_general(onehot, weight, (((1,), (1,)), ((), ())), preferred_element_type=F32)
    share = rows // NV
    picked, h = lax.optimization_barrier((picked.astype(BF16), h))
    picked = lax.all_to_all(
        picked.reshape(NV, share, feats), VOC, split_axis=0, concat_axis=0, tiled=True
    )
    target_w = jnp.sum(picked.astype(F32), axis=0)

    part = None
    for o in (0, 1, 3, 2):
        d = jnp.dot(h[:, o].reshape(NZ * per, feats), w[o], preferred_element_type=F32)
        part = d if part is None else part + d
    logits = line_scatter(part.reshape(NZ, per, width))

    mine = lax.dynamic_slice_in_dim(targets, (z * NX + x) * per, per, 0)
    top = jnp.max(logits, axis=1)
    e = jnp.exp(logits - top[:, None])
    total = jnp.sum(e, axis=1)
    hit = mine[:, None] == columns[None, :]
    goal = jnp.sum(jnp.where(hit, logits, F32(0.0)), axis=1)

    lanes = -(-width // 128) * 128
    pad = lanes - width - 9
    sent = jnp.concatenate(
        [e.astype(BF16), split3(top), split3(total), split3(goal), jnp.zeros((per, pad), BF16)], 1
    )
    got = jnp.concatenate(line_gather(sent), 0)
    probs = got[:, :width]
    stats = [join3(got[:, width + 3 * k : width + 3 * k + 3]) for k in range(3)]
    stats = jnp.stack(stats + [jnp.zeros_like(stats[0])] * (64 - 3), axis=1)

    pieces = []
    for o in range(NX):
        g = lax.dot_general(probs, w[o], (((1,), (1,)), ((), ())), preferred_element_type=F32)
        g = jnp.concatenate([g, stats], axis=1)
        if o:
            g = lax.ppermute(g, "x", [(i, (i + o) % NX) for i in range(NX)])
        pieces.append(g)
    grads = jnp.concatenate(pieces, 0)

    owner = source // per
    place = ((x - owner % NX) % NX) * (NZ * per) + ((z - owner // NX) % NZ) * per + source % per
    grads = jnp.take(grads, place, axis=0, mode="clip")
    st = grads[:, feats : feats + 3].T
    dp_rows = lax.dynamic_slice_in_dim(st, (z * NX + x) * per, per, 1)
    extra = jnp.concatenate(
        [
            jnp.pad(st[:2].reshape(2, NV, share).transpose(1, 0, 2), ((0, 0), (0, 0), (0, feats - share))),
            jnp.broadcast_to(jnp.pad(dp_rows, ((0, 3), (0, feats - per)))[None], (NV, 6, feats)),
        ],
        axis=1,
    )
    msg = jnp.concatenate([grads[:, :feats].reshape(NV, share, feats), extra], axis=1)
    msg = lax.all_to_all(msg, VOC, split_axis=0, concat_axis=0, tiled=True)

    tops, totals = msg[:, share, :share], msg[:, share + 1, :share]
    peak = jnp.max(tops, axis=0)
    scale = jnp.exp(tops - peak[None])
    norm = jnp.sum(scale * totals, axis=0)
    mixed = jnp.sum(scale[:, :, None] * msg[:, :share], axis=0) / norm[:, None]
    my_coef = lax.dynamic_slice_in_dim(coef, v * share, share, 0)
    hidden_grad = my_coef[:, None] * (mixed - target_w)

    tops, totals, goals = (msg[:, share + 2 + k, :per] for k in range(3))
    peak = jnp.max(tops, axis=0)
    norm = jnp.sum(jnp.exp(tops - peak[None]) * totals, axis=0)
    logprob = jnp.sum(goals, axis=0) - (peak + jnp.log(norm))
    return (logprob, hidden_grad.astype(BF16))


def solution(mesh):
    fine = Mesh(mesh.devices.reshape(NZ, NX, NY, NH, NC), ("zl", "x") + VOC)
    dp = ("zl", "x")
    placed = (P(dp, None), P(dp, VOC), P(), P(), P(), P())
    return jax.shard_map(
        body, mesh=fine, in_specs=placed, out_specs=(P(dp), P(VOC, dp)), check_vma=False
    )
```

time: 747 us -> 274 us (0.37)
  the two profiles are of different devices: /device:TPU:2 before, /device:TPU:328 now
where the time goes in v1:
time: 274 us; the launch traced here: 273 us
  waiting for transfers between devices  123 us (45%)
  starting transfers between devices  107 us (39%)
  local copies, waits for them, and re-layouts  26 us (9%)
  matrix products  10.6 us (4%)
  other arithmetic  5.86 us (2%)
    ppermute x5, waiting for transfers between devices, line_gather(): lax.ppermute(right[-1], 'zl', [(i, i + 1) for i in range(s - 1, NZ - 1)])  36.5 us
    ppermute x5, starting transfers between devices, line_scatter(): left = lax.ppermute(to_left, 'zl', [(i, i - 1) for i in range(NZ - s, NZ)])  35.7 us
    all_to_all x1, waiting for transfers between devices, body(): msg = lax.all_to_all(msg, VOC, split_axis=0, concat_axis=0, tiled=True)  33.2 us
    ppermute x5, waiting for transfers between devices, line_scatter(): left = lax.ppermute(to_left, 'zl', [(i, i - 1) for i in range(NZ - s, NZ)])  24.3 us
    all_to_all x1, starting transfers between devices, body(): msg = lax.all_to_all(msg, VOC, split_axis=0, concat_axis=0, tiled=True)  11.7 us
    all_to_all x1, starting transfers between devices, body(): lax.all_to_all(picked.reshape(NV, share, feats), VOC, split_axis=0, conca...  9.55 us
    ppermute x3, starting transfers between devices, body(): g = lax.ppermute(g, 'x', [(i, (i + o) % NX) for i in range(NX)])  9.15 us
    all_to_all x1, starting transfers between devices, body(): h = lax.all_to_all(h, 'zl', split_axis=0, concat_axis=0, tiled=True)  8.1 us
  transfers between devices with their start and end apart: 30, of which 16 were waited for; matrix products, arithmetic and copies ran while one was open for 12% of the time, Pallas kernels for 0%

profile of v1, /device:TPU:328, one launch (start us, length us, event | category | flops | bytes accessed | tf_op | source)
XLA Modules:
  0.0 273.2 jit_solution(6795007136391696180)
XLA Ops:
  0.7 1.4 reshape.419
  2.9 8.1 %all-to-all-start = ((bf16[6,4,32,192]{3,1,2,0:T(4,128)(2,1)}), bf16[6,4,32,192]{3,1,2,0:T(4,128)(2,1)S(1)}, u32[]{:S(2)}, u32[]{:S(2)}) async-start(bf16[6,4,32,192]{3,1,2,0:T(4,128)(2,1)} %copy.58), calls=%async_computation | async-start | bytes 786432 | tf_op jit(solution)/shard_map/all_to_all | solution.py:66
  11.0 4.7 %collective-permute-start = (bf16[192,2376]{1,0:T(8,128)(2,1)}, bf16[192,2376]{1,0:T(8,128)(2,1)S(1)}, u32[]{:S(2)}, u32[]{:S(2)}) collective-permute-start(bf16[192,2376]{1,0:T(8,128)(2,1)} %param.7), channel_id=1, source_target_pairs={{0,96},{32,0},{64,32},{96,64},{1,97},{33,1},{65,33},{97,65},{2,98}... | collective-permute-start | bytes 2737160 | tf_op jit(solution)/shard_map/ppermute | solution.py:58
  15.7 1.9 collective-permute-start.1
  17.7 5.0 %gather_fusion = s32[768]{0:T(1024)S(1)} fusion(s32[192]{0:T(256)S(1)} %copy-done.1, s32[1024]{0:T(1024)S(1)} %pad_clamp_fusion.3), kind=kCustom, calls=%fused_computation | custom fusion | bytes 9216 | tf_op jit(solution)/shard_map/gather | solution.py:70
  22.8 3.2 %gather_fusion.1 = s32[768]{0:T(1024)S(1)} fusion(s32[768]{0:T(1024)S(1)} %copy-done.3, s32[1024]{0:T(1024)S(1)} %get-tuple-element.46), kind=kCustom, calls=%fused_computation.1 | custom fusion | bytes 9216 | tf_op jit(solution)/shard_map/gather | solution.py:72
  26.0 3.4 %fusion.5 = bf16[768,192]{0,1:T(8,128)(2,1)} fusion(bf16[192,2376]{1,0:T(8,128)(2,1)} %param.7, s32[2376]{0:T(1024)S(1)} %iota_add_fusion, s32[768]{0:T(1024)S(1)} %gather_fusion.1), kind=kOutput, calls=%fused_computation.14 | convolution fusion | flops 702683136 | bytes 1219872 | tf_op jit(solution)/shard_map/dot_general | solution.py:78
  29.9 5.5 %collective-permute-done = bf16[192,2376]{1,0:T(8,128)(2,1)S(1)} collective-permute-done((bf16[192,2376]{1,0:T(8,128)(2,1)}, bf16[192,2376]{1,0:T(8,128)(2,1)S(1)}, u32[]{:S(2)}, u32[]{:S(2)}) %collective-permute-start) | collective-permute-done | bytes 912416 | tf_op jit(solution)/shard_map/ppermute | solution.py:58
  35.4 5.5 %collective-permute-start.2 = (bf16[96,2376]{1,0:T(8,128)(2,1)S(1)}, bf16[96,2376]{1,0:T(8,128)(2,1)S(1)}, u32[]{:S(2)}, u32[]{:S(2)}) collective-permute-start(bf16[96,2376]{1,0:T(8,128)(2,1)S(1)} %slice.157), channel_id=1, source_target_pairs={{0,96},{32,0},{64,32},{96,64},{1,97},{33,1},{65,33},{97,65},{2,98}... | collective-permute-start | bytes 1368584 | tf_op jit(solution)/shard_map/ppermute | solution.py:61
  40.9 1.6 fusion.49
  42.6 1.9 collective-permute-start.3
  44.9 4.5 %collective-permute-done.2 = bf16[96,2376]{1,0:T(8,128)(2,1)S(1)} collective-permute-done((bf16[96,2376]{1,0:T(8,128)(2,1)S(1)}, bf16[96,2376]{1,0:T(8,128)(2,1)S(1)}, u32[]{:S(2)}, u32[]{:S(2)}) %collective-permute-start.2) | collective-permute-done | bytes 456224 | tf_op jit(solution)/shard_map/ppermute | solution.py:61
  49.5 6.9 %collective-permute-done.3 = bf16[96,2376]{1,0:T(8,128)(2,1)S(1)} collective-permute-done((bf16[96,2376]{1,0:T(8,128)(2,1)S(1)}, bf16[96,2376]{1,0:T(8,128)(2,1)S(1)}, u32[]{:S(2)}, u32[]{:S(2)}) %collective-permute-start.3) | collective-permute-done | bytes 456224 | tf_op jit(solution)/shard_map/ppermute | solution.py:61
  60.1 2.5 collective-permute-start.9
  62.6 4.4 %collective-permute-done.9 = f32[32,2376]{1,0:T(8,128)S(1)} collective-permute-done((f32[32,2376]{1,0:T(8,128)S(1)}, f32[32,2376]{1,0:T(8,128)S(1)}, u32[]{:S(2)}, u32[]{:S(2)}) %collective-permute-start.9) | collective-permute-done | bytes 304160 | tf_op jit(solution)/shard_map/ppermute | solution.py:35
  67.0 4.4 %collective-permute-start.10 = (f32[32,2376]{1,0:T(8,128)S(1)}, f32[32,2376]{1,0:T(8,128)S(1)}, u32[]{:S(2)}, u32[]{:S(2)}) collective-permute-start(f32[32,2376]{1,0:T(8,128)S(1)} %get-tuple-element.18), channel_id=1, source_target_pairs={{512,384},{640,512},{513,385},{641,513},{514,386},{642,514},{515,3... | collective-permute-start | bytes 912392 | tf_op jit(solution)/shard_map/ppermute | solution.py:35
  71.4 4.4 %collective-permute-done.10 = f32[32,2376]{1,0:T(8,128)S(1)} collective-permute-done((f32[32,2376]{1,0:T(8,128)S(1)}, f32[32,2376]{1,0:T(8,128)S(1)}, u32[]{:S(2)}, u32[]{:S(2)}) %collective-permute-start.10) | collective-permute-done | bytes 304160 | tf_op jit(solution)/shard_map/ppermute | solution.py:35
  75.8 16.5 %collective-permute-start.11 = (f32[32,2376]{1,0:T(8,128)S(1)}, f32[32,2376]{1,0:T(8,128)S(1)}, u32[]{:S(2)}, u32[]{:S(2)}) collective-permute-start(f32[32,2376]{1,0:T(8,128)S(1)} %slice_add_fusion.3), channel_id=1, source_target_pairs={{384,256},{512,384},{640,512},{385,257},{513,385},{641,513},{386,2... | collective-permute-start | bytes 912392 | tf_op jit(solution)/shard_map/ppermute | solution.py:35
  93.0 5.7 %collective-permute-done.11 = f32[32,2376]{1,0:T(8,128)S(1)} collective-permute-done((f32[32,2376]{1,0:T(8,128)S(1)}, f32[32,2376]{1,0:T(8,128)S(1)}, u32[]{:S(2)}, u32[]{:S(2)}) %collective-permute-start.11) | collective-permute-done | bytes 304160 | tf_op jit(solution)/shard_map/ppermute | solution.py:35
  98.8 5.9 %collective-permute-start.12 = (f32[32,2376]{1,0:T(8,128)S(1)}, f32[32,2376]{1,0:T(8,128)S(1)}, u32[]{:S(2)}, u32[]{:S(2)}) collective-permute-start(f32[32,2376]{1,0:T(8,128)S(1)} %slice_add_fusion.1), channel_id=1, source_target_pairs={{256,128},{384,256},{512,384},{640,512},{257,129},{385,257},{513,3... | collective-permute-start | bytes 912392 | tf_op jit(solution)/shard_map/ppermute | solution.py:35
  104.7 7.5 %collective-permute-done.12 = f32[32,2376]{1,0:T(8,128)S(1)} collective-permute-done((f32[32,2376]{1,0:T(8,128)S(1)}, f32[32,2376]{1,0:T(8,128)S(1)}, u32[]{:S(2)}, u32[]{:S(2)}) %collective-permute-start.12) | collective-permute-done | bytes 304160 | tf_op jit(solution)/shard_map/ppermute | solution.py:35
  112.3 6.4 %collective-permute-start.13 = (f32[32,2376]{1,0:T(8,128)S(1)}, f32[32,2376]{1,0:T(8,128)}, u32[]{:S(2)}, u32[]{:S(2)}) collective-permute-start(f32[32,2376]{1,0:T(8,128)S(1)} %get-tuple-element.16), channel_id=1, source_target_pairs={{128,0},{256,128},{384,256},{512,384},{640,512},{129,1},{257,129},... | collective-permute-start | bytes 912392 | tf_op jit(solution)/shard_map/ppermute | solution.py:35
  118.7 1.3 collective-permute-start.8
  120.1 2.3 collective-permute-done.13
  122.4 7.8 %collective-permute-done.8 = f32[32,2376]{1,0:T(8,128)} collective-permute-done((f32[32,2376]{1,0:T(8,128)S(1)}, f32[32,2376]{1,0:T(8,128)}, u32[]{:S(2)}, u32[]{:S(2)}) %collective-permute-start.8) | collective-permute-done | bytes 304160 | tf_op jit(solution)/shard_map/ppermute | solution.py:34
  132.8 5.1 %collective-permute-start.15 = (bf16[32,2432]{1,0:T(8,128)(2,1)S(1)}, bf16[32,2432]{1,0:T(8,128)(2,1)S(1)}, u32[]{:S(2)}, u32[]{:S(2)}) collective-permute-start(bf16[32,2432]{1,0:T(8,128)(2,1)S(1)} %concatenate.41), channel_id=1, source_target_pairs={{128,0},{256,128},{384,256},{512,384},{640,512},{129,1},{257,129},... | collective-permute-start | bytes 466952 | tf_op jit(solution)/shard_map/ppermute | solution.py:43
  138.0 1.3 collective-permute-start.14
  139.3 1.4 collective-permute-done.15
  141.4 5.1 %collective-permute-done.14 = bf16[32,2432]{1,0:T(8,128)(2,1)S(1)} collective-permute-done((bf16[32,2432]{1,0:T(8,128)(2,1)S(1)}, bf16[32,2432]{1,0:T(8,128)(2,1)S(1)}, u32[]{:S(2)}, u32[]{:S(2)}) %collective-permute-start.14) | collective-permute-done | bytes 155680 | tf_op jit(solution)/shard_map/ppermute | solution.py:42
  146.5 1.3 collective-permute-start.20
  148.5 5.1 %collective-permute-done.20 = bf16[32,2432]{1,0:T(8,128)(2,1)S(1)} collective-permute-done((bf16[32,2432]{1,0:T(8,128)(2,1)S(1)}, bf16[32,2432]{1,0:T(8,128)(2,1)S(1)}, u32[]{:S(2)}, u32[]{:S(2)}) %collective-permute-start.20) | collective-permute-done | bytes 155680 | tf_op jit(solution)/shard_map/ppermute | solution.py:42
  153.6 1.3 collective-permute-start.21
  156.5 9.6 %all-to-all-start.2 = ((bf16[32,24,192]{2,1,0:T(8,128)(2,1)}), bf16[32,24,192]{2,1,0:T(8,128)(2,1)S(1)}, u32[]{:S(2)}, u32[]{:S(2)}) async-start(bf16[32,24,192]{2,1,0:T(8,128)(2,1)} %bitcast.17), calls=%async_computation.2 | async-start | bytes 786432 | tf_op jit(solution)/shard_map/all_to_all | solution.py:81
  166.1 1.4 collective-permute-start.22
  168.3 10.5 %collective-permute-done.22 = bf16[32,2432]{1,0:T(8,128)(2,1)S(1)} collective-permute-done((bf16[32,2432]{1,0:T(8,128)(2,1)S(1)}, bf16[32,2432]{1,0:T(8,128)(2,1)S(1)}, u32[]{:S(2)}, u32[]{:S(2)}) %collective-permute-start.22) | collective-permute-done | bytes 155680 | tf_op jit(solution)/shard_map/ppermute | solution.py:42
  178.8 1.3 collective-permute-start.23
  180.3 15.7 %collective-permute-done.23 = bf16[32,2432]{1,0:T(8,128)(2,1)S(1)} collective-permute-done((bf16[32,2432]{1,0:T(8,128)(2,1)S(1)}, bf16[32,2432]{1,0:T(8,128)(2,1)S(1)}, u32[]{:S(2)}, u32[]{:S(2)}) %collective-permute-start.23) | collective-permute-done | bytes 155680 | tf_op jit(solution)/shard_map/ppermute | solution.py:42
  198.4 1.9 collective-permute-start.24
  200.6 2.9 %collective-permute-start.25 = (f32[192,256]{1,0:T(8,128)S(1)}, f32[192,256]{1,0:T(8,128)S(1)}, u32[]{:S(2)}, u32[]{:S(2)}) collective-permute-start(f32[192,256]{1,0:T(8,128)S(1)} %concatenate.45), channel_id=1, source_target_pairs={{0,64},{32,96},{64,0},{96,32},{1,65},{33,97},{65,1},{97,33},{2,66}... | collective-permute-start | bytes 589832 | tf_op jit(solution)/shard_map/ppermute | solution.py:114
  203.6 1.6 fusion.11
  205.5 4.3 %collective-permute-start.26 = (f32[192,256]{1,0:T(8,128)S(1)}, f32[192,256]{1,0:T(8,128)S(1)}, u32[]{:S(2)}, u32[]{:S(2)}) collective-permute-start(f32[192,256]{1,0:T(8,128)S(1)} %concatenate.46), channel_id=1, source_target_pairs={{0,96},{32,0},{64,32},{96,64},{1,97},{33,1},{65,33},{97,65},{2,98}... | collective-permute-start | bytes 589832 | tf_op jit(solution)/shard_map/ppermute | solution.py:114
  209.8 1.9 fusion.17
  212.0 2.4 collective-permute-done.26
  214.5 2.1 gather_fusion.2
  218.4 11.7 %all-to-all-start.1 = ((f32[32,32,192]{2,1,0:T(8,128)}), f32[32,32,192]{2,1,0:T(8,128)S(1)}, u32[]{:S(2)}, u32[]{:S(2)}) async-start(f32[32,32,192]{2,1,0:T(8,128)} %fusion.8), calls=%async_computation.1 | async-start | bytes 2097152 | tf_op jit(solution)/shard_map/all_to_all | solution.py:131
  230.1 3.2 %gather_fusion.4 = f32[768]{0:T(1024)S(1)} fusion(f32[768]{0:T(1024)S(1)} %copy-done, s32[1024]{0:T(1024)S(1)} %get-tuple-element.46), kind=kCustom, calls=%fused_computation.4 | custom fusion | bytes 9216 | tf_op jit(solution)/shard_map/gather | solution.py:74
  233.3 5.0 %gather_fusion.3 = s32[768]{0:T(1024)S(1)} fusion(s32[192]{0:T(256)S(1)} %copy-done.2, s32[1024]{0:T(1024)S(1)} %get-tuple-element.45), kind=kCustom, calls=%fused_computation.3 | custom fusion | bytes 9216 | tf_op jit(solution)/shard_map/gather | solution.py:73
  238.5 33.2 %all-to-all-done.1 = f32[32,32,192]{2,1,0:T(8,128)S(1)} async-done(((f32[32,32,192]{2,1,0:T(8,128)}), f32[32,32,192]{2,1,0:T(8,128)S(1)}, u32[]{:S(2)}, u32[]{:S(2)}) %all-to-all-start.1) | async-done | bytes 786464 | tf_op jit(solution)/shard_map/all_to_all | solution.py:131
  (126 shorter events, 19.6 us)
Async XLA Ops:
  0.6 229.4 %copy-start = (f32[768]{0:T(1024)S(1)}, f32[768]{0:T(1024)}, u32[]{:S(2)}) copy-start(f32[768]{0:T(1024)} %param.9) | copy-start | bytes 9220
  0.6 17.0 %copy-start.1 = (s32[192]{0:T(256)S(1)}, s32[192]{0:T(256)}, u32[]{:S(2)}) copy-start(s32[192]{0:T(256)} %param.11) | copy-start | bytes 2308
  2.9 26.5 %all-to-all-start = ((bf16[6,4,32,192]{3,1,2,0:T(4,128)(2,1)}), bf16[6,4,32,192]{3,1,2,0:T(4,128)(2,1)S(1)}, u32[]{:S(2)}, u32[]{:S(2)}) async-start(bf16[6,4,32,192]{3,1,2,0:T(4,128)(2,1)} %copy.58), calls=%async_computation | async-start | bytes 786432 | tf_op jit(solution)/shard_map/all_to_all | solution.py:66
  11.0 24.4 %collective-permute-start = (bf16[192,2376]{1,0:T(8,128)(2,1)}, bf16[192,2376]{1,0:T(8,128)(2,1)S(1)}, u32[]{:S(2)}, u32[]{:S(2)}) collective-permute-start(bf16[192,2376]{1,0:T(8,128)(2,1)} %param.7), channel_id=1, source_target_pairs={{0,96},{32,0},{64,32},{96,64},{1,97},{33,1},{65,33},{97,65},{2,98}... | collective-permute-start | bytes 2737160 | tf_op jit(solution)/shard_map/ppermute | solution.py:58
  15.7 26.8 %collective-permute-start.1 = (bf16[192,2376]{1,0:T(8,128)(2,1)}, bf16[192,2376]{1,0:T(8,128)(2,1)S(1)}, u32[]{:S(2)}, u32[]{:S(2)}) collective-permute-start(bf16[192,2376]{1,0:T(8,128)(2,1)} %param.7), channel_id=1, source_target_pairs={{0,32},{32,64},{64,96},{96,0},{1,33},{33,65},{65,97},{97,1},{2,34}... | collective-permute-start | bytes 2737160 | tf_op jit(solution)/shard_map/ppermute | solution.py:59
  17.7 5.1 %copy-start.3 = (s32[768]{0:T(1024)S(1)}, s32[768]{0:T(1024)}, u32[]{:S(2)}) copy-start(s32[768]{0:T(1024)} %param.8) | copy-start | bytes 9220
  35.4 9.1 %copy-start.4 = (bf16[192,2376]{1,0:T(8,128)(2,1)}, bf16[192,2376]{1,0:T(8,128)(2,1)S(1)}, u32[]{:S(2)}) copy-start(bf16[192,2376]{1,0:T(8,128)(2,1)S(1)} %collective-permute-done) | copy-start | bytes 2737156
  35.4 14.0 %collective-permute-start.2 = (bf16[96,2376]{1,0:T(8,128)(2,1)S(1)}, bf16[96,2376]{1,0:T(8,128)(2,1)S(1)}, u32[]{:S(2)}, u32[]{:S(2)}) collective-permute-start(bf16[96,2376]{1,0:T(8,128)(2,1)S(1)} %slice.157), channel_id=1, source_target_pairs={{0,96},{32,0},{64,32},{96,64},{1,97},{33,1},{65,33},{97,65},{2,98}... | collective-permute-start | bytes 1368584 | tf_op jit(solution)/shard_map/ppermute | solution.py:61
  42.6 13.8 %collective-permute-start.3 = (bf16[96,2376]{1,0:T(8,128)(2,1)S(1)}, bf16[96,2376]{1,0:T(8,128)(2,1)S(1)}, u32[]{:S(2)}, u32[]{:S(2)}) collective-permute-start(bf16[96,2376]{1,0:T(8,128)(2,1)S(1)} %slice.158), channel_id=1, source_target_pairs={{0,32},{32,64},{64,96},{96,0},{1,33},{33,65},{65,97},{97,1},{2,34}... | collective-permute-start | bytes 1368584 | tf_op jit(solution)/shard_map/ppermute | solution.py:61
  56.5 1.0 copy-start.6
  57.9 0.7 collective-permute-start.4
  58.6 0.7 collective-permute-start.5
  59.4 3.2 %collective-permute-start.6 = (f32[32,2376]{1,0:T(8,128)S(1)}, f32[32,2376]{1,0:T(8,128)S(1)}, u32[]{:S(2)}, u32[]{:S(2)}) collective-permute-start(f32[32,2376]{1,0:T(8,128)S(1)} %get-tuple-element.19), channel_id=1, source_target_pairs={{0,128},{128,256},{256,384},{1,129},{129,257},{257,385},{2,130},{1... | collective-permute-start | bytes 912392 | tf_op jit(solution)/shard_map/ppermute | solution.py:34
  60.1 6.9 %collective-permute-start.9 = (f32[32,2376]{1,0:T(8,128)S(1)}, f32[32,2376]{1,0:T(8,128)S(1)}, u32[]{:S(2)}, u32[]{:S(2)}) collective-permute-start(f32[32,2376]{1,0:T(8,128)S(1)} %get-tuple-element.20), channel_id=1, source_target_pairs={{640,512},{641,513},{642,514},{643,515},{644,516},{645,517},{646,5... | collective-permute-start | bytes 912392 | tf_op jit(solution)/shard_map/ppermute | solution.py:35
  67.0 8.8 %collective-permute-start.10 = (f32[32,2376]{1,0:T(8,128)S(1)}, f32[32,2376]{1,0:T(8,128)S(1)}, u32[]{:S(2)}, u32[]{:S(2)}) collective-permute-start(f32[32,2376]{1,0:T(8,128)S(1)} %get-tuple-element.18), channel_id=1, source_target_pairs={{512,384},{640,512},{513,385},{641,513},{514,386},{642,514},{515,3... | collective-permute-start | bytes 912392 | tf_op jit(solution)/shard_map/ppermute | solution.py:35
  75.8 22.9 %collective-permute-start.11 = (f32[32,2376]{1,0:T(8,128)S(1)}, f32[32,2376]{1,0:T(8,128)S(1)}, u32[]{:S(2)}, u32[]{:S(2)}) collective-permute-start(f32[32,2376]{1,0:T(8,128)S(1)} %slice_add_fusion.3), channel_id=1, source_target_pairs={{384,256},{512,384},{640,512},{385,257},{513,385},{641,513},{386,2... | collective-permute-start | bytes 912392 | tf_op jit(solution)/shard_map/ppermute | solution.py:35
  92.3 12.4 %collective-permute-start.7 = (f32[32,2376]{1,0:T(8,128)S(1)}, f32[32,2376]{1,0:T(8,128)S(1)}, u32[]{:S(2)}, u32[]{:S(2)}) collective-permute-start(f32[32,2376]{1,0:T(8,128)S(1)} %get-tuple-element.17), channel_id=1, source_target_pairs={{0,128},{128,256},{256,384},{384,512},{1,129},{129,257},{257,385},... | collective-permute-start | bytes 912392 | tf_op jit(solution)/shard_map/ppermute | solution.py:34
  98.8 13.4 %collective-permute-start.12 = (f32[32,2376]{1,0:T(8,128)S(1)}, f32[32,2376]{1,0:T(8,128)S(1)}, u32[]{:S(2)}, u32[]{:S(2)}) collective-permute-start(f32[32,2376]{1,0:T(8,128)S(1)} %slice_add_fusion.1), channel_id=1, source_target_pairs={{256,128},{384,256},{512,384},{640,512},{257,129},{385,257},{513,3... | collective-permute-start | bytes 912392 | tf_op jit(solution)/shard_map/ppermute | solution.py:35
  112.3 10.1 %collective-permute-start.13 = (f32[32,2376]{1,0:T(8,128)S(1)}, f32[32,2376]{1,0:T(8,128)}, u32[]{:S(2)}, u32[]{:S(2)}) collective-permute-start(f32[32,2376]{1,0:T(8,128)S(1)} %get-tuple-element.16), channel_id=1, source_target_pairs={{128,0},{256,128},{384,256},{512,384},{640,512},{129,1},{257,129},... | collective-permute-start | bytes 912392 | tf_op jit(solution)/shard_map/ppermute | solution.py:35
  118.7 11.5 %collective-permute-start.8 = (f32[32,2376]{1,0:T(8,128)S(1)}, f32[32,2376]{1,0:T(8,128)}, u32[]{:S(2)}, u32[]{:S(2)}) collective-permute-start(f32[32,2376]{1,0:T(8,128)S(1)} %get-tuple-element.15), channel_id=1, source_target_pairs={{0,128},{128,256},{256,384},{384,512},{512,640},{1,129},{129,257},... | collective-permute-start | bytes 912392 | tf_op jit(solution)/shard_map/ppermute | solution.py:34
  122.4 33.2 %copy-start.8 = (bf16[768,192]{0,1:T(8,128)(2,1)S(1)}, bf16[768,192]{0,1:T(8,128)(2,1)}, u32[]{:S(2)}) copy-start(bf16[768,192]{0,1:T(8,128)(2,1)} %fusion.5) | copy-start | bytes 884740
  132.8 7.9 %collective-permute-start.15 = (bf16[32,2432]{1,0:T(8,128)(2,1)S(1)}, bf16[32,2432]{1,0:T(8,128)(2,1)S(1)}, u32[]{:S(2)}, u32[]{:S(2)}) collective-permute-start(bf16[32,2432]{1,0:T(8,128)(2,1)S(1)} %concatenate.41), channel_id=1, source_target_pairs={{128,0},{256,128},{384,256},{512,384},{640,512},{129,1},{257,129},... | collective-permute-start | bytes 466952 | tf_op jit(solution)/shard_map/ppermute | solution.py:43
  138.0 8.5 %collective-permute-start.14 = (bf16[32,2432]{1,0:T(8,128)(2,1)S(1)}, bf16[32,2432]{1,0:T(8,128)(2,1)S(1)}, u32[]{:S(2)}, u32[]{:S(2)}) collective-permute-start(bf16[32,2432]{1,0:T(8,128)(2,1)S(1)} %concatenate.41), channel_id=1, source_target_pairs={{0,128},{128,256},{256,384},{384,512},{512,640},{1,129},{129,257},... | collective-permute-start | bytes 466952 | tf_op jit(solution)/shard_map/ppermute | solution.py:42
  140.7 7.1 %collective-permute-start.16 = (bf16[32,2432]{1,0:T(8,128)(2,1)S(1)}, bf16[32,2432]{1,0:T(8,128)(2,1)S(1)}, u32[]{:S(2)}, u32[]{:S(2)}) collective-permute-start(bf16[32,2432]{1,0:T(8,128)(2,1)S(1)} %collective-permute-done.15), channel_id=1, source_target_pairs={{128,0},{256,128},{384,256},{512,384},{129,1},{257,129},{385,257},... | collective-permute-start | bytes 466952 | tf_op jit(solution)/shard_map/ppermute | solution.py:43
  146.5 7.1 %collective-permute-start.20 = (bf16[32,2432]{1,0:T(8,128)(2,1)S(1)}, bf16[32,2432]{1,0:T(8,128)(2,1)S(1)}, u32[]{:S(2)}, u32[]{:S(2)}) collective-permute-start(bf16[32,2432]{1,0:T(8,128)(2,1)S(1)} %collective-permute-done.14), channel_id=1, source_target_pairs={{128,256},{256,384},{384,512},{512,640},{129,257},{257,385},{385,5... | collective-permute-start | bytes 466952 | tf_op jit(solution)/shard_map/ppermute | solution.py:42
  147.8 7.1 %collective-permute-start.17 = (bf16[32,2432]{1,0:T(8,128)(2,1)S(1)}, bf16[32,2432]{1,0:T(8,128)(2,1)S(1)}, u32[]{:S(2)}, u32[]{:S(2)}) collective-permute-start(bf16[32,2432]{1,0:T(8,128)(2,1)S(1)} %collective-permute-done.16), channel_id=1, source_target_pairs={{128,0},{256,128},{384,256},{129,1},{257,129},{385,257},{130,2},{2... | collective-permute-start | bytes 466952 | tf_op jit(solution)/shard_map/ppermute | solution.py:43
  153.6 12.5 %collective-permute-start.21 = (bf16[32,2432]{1,0:T(8,128)(2,1)S(1)}, bf16[32,2432]{1,0:T(8,128)(2,1)S(1)}, u32[]{:S(2)}, u32[]{:S(2)}) collective-permute-start(bf16[32,2432]{1,0:T(8,128)(2,1)S(1)} %collective-permute-done.20), channel_id=1, source_target_pairs={{256,384},{384,512},{512,640},{257,385},{385,513},{513,641},{258,3... | collective-permute-start | bytes 466952 | tf_op jit(solution)/shard_map/ppermute | solution.py:42
  154.9 12.7 %collective-permute-start.18 = (bf16[32,2432]{1,0:T(8,128)(2,1)S(1)}, bf16[32,2432]{1,0:T(8,128)(2,1)S(1)}, u32[]{:S(2)}, u32[]{:S(2)}) collective-permute-start(bf16[32,2432]{1,0:T(8,128)(2,1)S(1)} %collective-permute-done.17), channel_id=1, source_target_pairs={{128,0},{256,128},{129,1},{257,129},{130,2},{258,130},{131,3},{259... | collective-permute-start | bytes 466952 | tf_op jit(solution)/shard_map/ppermute | solution.py:43
  156.5 61.8 %all-to-all-start.2 = ((bf16[32,24,192]{2,1,0:T(8,128)(2,1)}), bf16[32,24,192]{2,1,0:T(8,128)(2,1)S(1)}, u32[]{:S(2)}, u32[]{:S(2)}) async-start(bf16[32,24,192]{2,1,0:T(8,128)(2,1)} %bitcast.17), calls=%async_computation.2 | async-start | bytes 786432 | tf_op jit(solution)/shard_map/all_to_all | solution.py:81
  166.1 30.1 %copy-start.7 = (bf16[192,2376]{1,0:T(8,128)(2,1)S(1)}, bf16[192,2376]{1,0:T(8,128)(2,1)}, u32[]{:S(2)}) copy-start(bf16[192,2376]{1,0:T(8,128)(2,1)} %copy-done.6) | copy-start | bytes 2737156
  166.1 12.7 %collective-permute-start.22 = (bf16[32,2432]{1,0:T(8,128)(2,1)S(1)}, bf16[32,2432]{1,0:T(8,128)(2,1)S(1)}, u32[]{:S(2)}, u32[]{:S(2)}) collective-permute-start(bf16[32,2432]{1,0:T(8,128)(2,1)S(1)} %collective-permute-done.21), channel_id=1, source_target_pairs={{384,512},{512,640},{385,513},{513,641},{386,514},{514,642},{387,5... | collective-permute-start | bytes 466952 | tf_op jit(solution)/shard_map/ppermute | solution.py:42
  167.6 12.5 %collective-permute-start.19 = (bf16[32,2432]{1,0:T(8,128)(2,1)S(1)}, bf16[32,2432]{1,0:T(8,128)(2,1)S(1)}, u32[]{:S(2)}, u32[]{:S(2)}) collective-permute-start(bf16[32,2432]{1,0:T(8,128)(2,1)S(1)} %collective-permute-done.18), channel_id=1, source_target_pairs={{128,0},{129,1},{130,2},{131,3},{132,4},{133,5},{134,6},{135,7},{1... | collective-permute-start | bytes 466952 | tf_op jit(solution)/shard_map/ppermute | solution.py:43
  178.8 17.2 %collective-permute-start.23 = (bf16[32,2432]{1,0:T(8,128)(2,1)S(1)}, bf16[32,2432]{1,0:T(8,128)(2,1)S(1)}, u32[]{:S(2)}, u32[]{:S(2)}) collective-permute-start(bf16[32,2432]{1,0:T(8,128)(2,1)S(1)} %collective-permute-done.22), channel_id=1, source_target_pairs={{512,640},{513,641},{514,642},{515,643},{516,644},{517,645},{518,6... | collective-permute-start | bytes 466952 | tf_op jit(solution)/shard_map/ppermute | solution.py:42
  196.1 2.1 copy-start.9
  196.1 1.5 copy-start.5
  198.4 13.6 %collective-permute-start.24 = (f32[192,256]{1,0:T(8,128)S(1)}, f32[192,256]{1,0:T(8,128)S(1)}, u32[]{:S(2)}, u32[]{:S(2)}) collective-permute-start(f32[192,256]{1,0:T(8,128)S(1)} %concatenate.44), channel_id=1, source_target_pairs={{0,32},{32,64},{64,96},{96,0},{1,33},{33,65},{65,97},{97,1},{2,34}... | collective-permute-start | bytes 589832 | tf_op jit(solution)/shard_map/ppermute | solution.py:114
  200.6 11.4 %collective-permute-start.25 = (f32[192,256]{1,0:T(8,128)S(1)}, f32[192,256]{1,0:T(8,128)S(1)}, u32[]{:S(2)}, u32[]{:S(2)}) collective-permute-start(f32[192,256]{1,0:T(8,128)S(1)} %concatenate.45), channel_id=1, source_target_pairs={{0,64},{32,96},{64,0},{96,32},{1,65},{33,97},{65,1},{97,33},{2,66}... | collective-permute-start | bytes 589832 | tf_op jit(solution)/shard_map/ppermute | solution.py:114
  205.5 9.0 %collective-permute-start.26 = (f32[192,256]{1,0:T(8,128)S(1)}, f32[192,256]{1,0:T(8,128)S(1)}, u32[]{:S(2)}, u32[]{:S(2)}) collective-permute-start(f32[192,256]{1,0:T(8,128)S(1)} %concatenate.46), channel_id=1, source_target_pairs={{0,96},{32,0},{64,32},{96,64},{1,97},{33,1},{65,33},{97,65},{2,98}... | collective-permute-start | bytes 589832 | tf_op jit(solution)/shard_map/ppermute | solution.py:114
  218.4 53.3 %all-to-all-start.1 = ((f32[32,32,192]{2,1,0:T(8,128)}), f32[32,32,192]{2,1,0:T(8,128)S(1)}, u32[]{:S(2)}, u32[]{:S(2)}) async-start(f32[32,32,192]{2,1,0:T(8,128)} %fusion.8), calls=%async_computation.1 | async-start | bytes 2097152 | tf_op jit(solution)/shard_map/all_to_all | solution.py:131
  230.1 3.2 %copy-start.2 = (s32[192]{0:T(256)S(1)}, s32[192]{0:T(256)}, u32[]{:S(2)}) copy-start(s32[192]{0:T(256)} %param.10) | copy-start | bytes 2308

commit v2 on v1

v2 whole, which is shorter than its diff:
```python
import jax
import jax.numpy as jnp
from jax import lax
from jax.sharding import Mesh, PartitionSpec as P

BLK = 4
NZ, NX, NY, NH, NC = 6, 4, 8, 2, 2
VOC = ("y", "zh", "c")
NV = NY * NH * NC
F32, BF16 = jnp.float32, jnp.bfloat16


def trade(a, axes):
    return lax.all_to_all(a, axes, split_axis=0, concat_axis=0, tiled=True)


def roll_to(a, axis, start):
    return lax.dynamic_slice_in_dim(jnp.concatenate([a, a], axis), start, a.shape[axis], axis)


def stat_lanes(stats, lanes):
    lane = lax.broadcasted_iota(jnp.int32, (stats[0].shape[0], lanes), 1)
    value = jnp.zeros(lane.shape, F32)
    for k, a in enumerate(stats):
        value = jnp.where(lane // 3 == k, a[:, None], value)
    hi = lax.reduce_precision(value, 8, 7)
    rest = value - hi
    mid = lax.reduce_precision(rest, 8, 7)
    return jnp.where(lane % 3 == 0, hi, jnp.where(lane % 3 == 1, mid, rest - mid)).astype(BF16)


def join3(cols):
    cols = cols.astype(F32)
    return (cols[:, 0] + cols[:, 1]) + cols[:, 2]


def line_scatter(part):
    right = left = None
    for s in range(1, NZ):
        to_right = part[NZ - s] if right is None else part[NZ - s] + right
        to_left = part[s] if left is None else part[s] + left
        to_right, to_left = lax.optimization_barrier((to_right, to_left))
        right = lax.ppermute(to_right, "zl", [(i, i + 1) for i in range(s)])
        left = lax.ppermute(to_left, "zl", [(i, i - 1) for i in range(NZ - s, NZ)])
    return part[0] + right + left


def line_gather(block):
    right, left = [block], [block]
    for s in range(1, NZ):
        r = lax.ppermute(right[-1], "zl", [(i, i + 1) for i in range(s - 1, NZ - 1)])
        l = lax.ppermute(left[-1], "zl", [(i, i - 1) for i in range(1, NZ - s + 1)])
        r, l = lax.optimization_barrier((r, l))
        right.append(r)
        left.append(l)
    z = lax.axis_index("zl")
    return [block] + [jnp.where(z >= q, right[q], left[NZ - q]) for q in range(1, NZ)]


def merge(a, b, feats):
    top = jnp.maximum(a[:, feats], b[:, feats])[:, None]
    fa, fb = jnp.exp(a[:, feats : feats + 1] - top), jnp.exp(b[:, feats : feats + 1] - top)
    summed = fa * a + fb * b
    goal = a[:, feats + 2] + b[:, feats + 2]
    return summed[:, :feats], top[:, 0], summed[:, feats + 1], goal


def body(hidden, weight, targets, advantage, counts, block_order):
    per, _ = hidden.shape
    feats, width = weight.shape
    rows = targets.shape[0]
    z, x, core = lax.axis_index("zl"), lax.axis_index("x"), lax.axis_index("c")
    v = lax.axis_index(VOC)
    share = rows // NV
    back = [(i, (i - 1) % NX) for i in range(NX)]
    forth = [(i, (i + 1) % NX) for i in range(NX)]
    swap = [(0, 1), (1, 0)]

    half = feats // 2
    up, down = weight[:half], weight[half:]
    u1, d3 = lax.ppermute(up, "x", back), lax.ppermute(down, "x", forth)
    d1, u3 = lax.ppermute(down, "x", back), lax.ppermute(up, "x", forth)
    u2, d2 = lax.ppermute(u1, "x", back), lax.ppermute(d3, "x", forth)
    w = [weight] + [jnp.concatenate(p, 0) for p in ((u1, d1), (u2, d2), (u3, d3))]

    h = hidden.reshape(per, NZ, NX, feats).transpose(1, 2, 0, 3)
    h = trade(h, "zl")
    h = roll_to(roll_to(h, 1, x), 0, z)

    k = jnp.arange(rows // NC, dtype=jnp.int32)
    pair = (k // share) * (NC * share) + k % share
    position = jnp.concatenate([pair + (1 - core) * share, pair + core * share])
    blocks = block_order[position // BLK]
    source = blocks * BLK + position % BLK
    wanted = targets[source]

    columns = v * width + jnp.arange(width, dtype=jnp.int32)
    onehot = (wanted[:, None] == columns[None, :]).astype(BF16)
    picked = lax.dot_general(onehot, weight, (((1,), (1,)), ((), ())), preferred_element_type=F32)
    picked = picked.astype(BF16)
    picked = picked[rows // NC :] + lax.ppermute(picked[: rows // NC], "c", swap)
    picked, h = lax.optimization_barrier((picked, h))
    picked = trade(picked.reshape(NY * NH, share, feats), ("y", "zh"))

    part = None
    for o in (0, 1, 3, 2):
        d = jnp.dot(h[:, o].reshape(NZ * per, feats), w[o], preferred_element_type=F32)
        part = d if part is None else part + d
    logits = line_scatter(part.reshape(NZ, per, width))

    mine = lax.dynamic_slice_in_dim(targets, (z * NX + x) * per, per, 0)
    top = jnp.max(logits, axis=1)
    e = jnp.exp(logits - top[:, None])
    total = jnp.sum(e, axis=1)
    hit = mine[:, None] == columns[None, :]
    goal = jnp.sum(jnp.where(hit, logits, F32(0.0)), axis=1)

    lanes = -(-width // 128) * 128
    sent = jnp.concatenate(
        [e.astype(BF16), stat_lanes((top, total, goal), lanes - width)], 1
    )
    got = jnp.concatenate(line_gather(sent), 0)
    probs = got[:, :width]
    stats = [join3(got[:, width + 3 * k : width + 3 * k + 3]) for k in range(3)]
    stats = jnp.stack(stats + [jnp.zeros_like(stats[0])] * (64 - 3), axis=1)

    pieces = [None] * NX
    for o in (2, 1, 3, 0):
        g = lax.dot_general(probs, w[o], (((1,), (1,)), ((), ())), preferred_element_type=F32)
        g = jnp.concatenate([g, stats], axis=1)
        pieces[o] = lax.ppermute(g, "x", [(i, (i + o) % NX) for i in range(NX)]) if o else g
    grads = jnp.concatenate(pieces, 0)

    here = (z * NX + x) * per
    own = here + jnp.arange(per, dtype=jnp.int32)
    own = block_order[own // BLK] * BLK + own % BLK
    order = jnp.concatenate([source[: rows // NC], own, source[rows // NC :], own])
    owner = order // per
    place = ((x - owner % NX) % NX) * (NZ * per) + ((z - owner // NX) % NZ) * per + order % per
    grads = jnp.take(grads, place, axis=0, mode="clip")
    cut = rows // NC + per
    grads, top, total, goal = merge(
        grads[cut:], lax.ppermute(grads[:cut], "c", swap), feats
    )
    nd = NY * NH
    kept = rows // NC
    by_dest = jnp.stack([a[:kept].reshape(nd, share) for a in (top, total)], axis=1)
    by_dest = jnp.pad(by_dest, ((0, 0), (0, 0), (0, feats - share)))
    by_row = jnp.stack([a[kept:] for a in (top, total, goal)])
    by_row = jnp.broadcast_to(jnp.pad(by_row, ((0, 3), (0, feats - per)))[None], (nd, 6, feats))
    msg = jnp.concatenate([grads[:kept].reshape(nd, share, feats), by_dest, by_row], axis=1)
    msg = lax.all_to_all(msg, ("y", "zh"), split_axis=0, concat_axis=0, tiled=True)

    spot = v * share + jnp.arange(share, dtype=jnp.int32)
    block = block_order[spot // BLK]
    alive = spot % BLK < counts[block]
    coef = jnp.where(alive, advantage[block * BLK + spot % BLK], F32(0.0))

    tops, totals = msg[:, share, :share], msg[:, share + 1, :share]
    peak = jnp.max(tops, axis=0)
    scale = jnp.exp(tops - peak[None])
    norm = jnp.sum(scale * totals, axis=0)
    mixed = jnp.sum(scale[:, :, None] * msg[:, :share], axis=0) / norm[:, None]
    target_w = jnp.sum(picked.astype(F32), axis=0)
    hidden_grad = coef[:, None] * (mixed - target_w)

    tops, totals, goals = (msg[:, share + 2 + k, :per] for k in range(3))
    peak = jnp.max(tops, axis=0)
    norm = jnp.sum(jnp.exp(tops - peak[None]) * totals, axis=0)
    logprob = jnp.sum(goals, axis=0) - (peak + jnp.log(norm))
    return (logprob, hidden_grad.astype(BF16))


def solution(mesh):
    fine = Mesh(mesh.devices.reshape(NZ, NX, NY, NH, NC), ("zl", "x") + VOC)
    dp = ("zl", "x")
    placed = (P(dp, None), P(dp, VOC), P(), P(), P(), P())

    return jax.shard_map(
        body, mesh=fine, in_specs=placed, out_specs=(P(dp), P(VOC, dp)), check_vma=False
    )
```

time: 274 us -> 268 us (0.978)
  the two profiles are of different devices: /device:TPU:328 before, /device:TPU:10 now
where the time goes in v2:
time: 268 us; the launch traced here: 266 us
  starting transfers between devices  116 us (43%)
  waiting for transfers between devices  101 us (38%)
  local copies, waits for them, and re-layouts  27.4 us (10%)
  other arithmetic  13.2 us (5%)
  matrix products  7.36 us (3%)
    ppermute x5, starting transfers between devices, line_scatter(): right = lax.ppermute(to_right, 'zl', [(i, i + 1) for i in range(s)])  32.8 us
    ppermute x5, waiting for transfers between devices, line_gather(): l = lax.ppermute(left[-1], 'zl', [(i, i - 1) for i in range(1, NZ - s + 1)])  31.4 us
    all_to_all x2, starting transfers between devices, trade(): return lax.all_to_all(a, axes, split_axis=0, concat_axis=0, tiled=True)  30.4 us
    all_to_all x1, waiting for transfers between devices, body(): lax.all_to_all(msg, ('y', 'zh'), split_axis=0, concat_axis=0, tiled=True)  19.4 us
    ppermute x5, waiting for transfers between devices, line_scatter(): right = lax.ppermute(to_right, 'zl', [(i, i + 1) for i in range(s)])  18.8 us
    all_to_all x2, waiting for transfers between devices, trade(): return lax.all_to_all(a, axes, split_axis=0, concat_axis=0, tiled=True)  16.5 us
    ppermute x3, starting transfers between devices, body(): lax.ppermute(g, 'x', [(i, (i + o) % NX) for i in range(NX)])  9.73 us
    ppermute x2, starting transfers between devices, body(): d1, u3 = (lax.ppermute(down, 'x', back), lax.ppermute(up, 'x', forth))  7.33 us
  transfers between devices with their start and end apart: 34, of which 18 were waited for; matrix products, arithmetic and copies ran while one was open for 10% of the time, Pallas kernels for 0%

profile of v2, /device:TPU:10, one launch (start us, length us, event | category | flops | bytes accessed | tf_op | source)
XLA Modules:
  0.0 266.1 jit_solution(4272613083672317002)
XLA Ops:
  0.7 2.0 fusion.59
  2.7 2.4 collective-permute-start.1
  5.3 5.0 %gather_fusion = s32[768]{0:T(1024)S(1)} fusion(s32[192]{0:T(256)S(1)} %copy-done.1, s32[1024]{0:T(1024)S(1)} %pad_clamp_fusion.6), kind=kCustom, calls=%fused_computation | custom fusion | bytes 9216 | tf_op jit(solution)/shard_map/gather | solution.py:93
  10.4 3.2 %gather_fusion.1 = s32[768]{0:T(1024)S(1)} fusion(s32[768]{0:T(1024)S(1)} %copy-done.2, s32[1024]{0:T(1024)S(1)} %get-tuple-element.93), kind=kCustom, calls=%fused_computation.1 | custom fusion | bytes 9216 | tf_op jit(solution)/shard_map/gather | solution.py:95
  13.6 1.5 fusion.4
  15.1 1.9 collective-permute-start
  17.1 4.7 %collective-permute-start.2 = (bf16[96,2376]{1,0:T(8,128)(2,1)}, bf16[96,2376]{1,0:T(8,128)(2,1)}, u32[]{:S(2)}, u32[]{:S(2)}) collective-permute-start(bf16[96,2376]{1,0:T(8,128)(2,1)} %get-tuple-element.70), channel_id=1, source_target_pairs={{0,96},{32,0},{64,32},{96,64},{1,97},{33,1},{65,33},{97,65},{2,98}... | collective-permute-start | bytes 1368584 | tf_op jit(solution)/shard_map/ppermute | solution.py:82
  21.7 1.9 collective-permute-start.4
  23.7 2.7 collective-permute-start.3
  27.6 12.1 %all-to-all-start = ((bf16[6,4,32,192]{3,1,2,0:T(4,128)(2,1)}), bf16[6,4,32,192]{3,1,2,0:T(4,128)(2,1)S(1)}, u32[]{:S(2)}, u32[]{:S(2)}) async-start(bf16[6,4,32,192]{3,1,2,0:T(4,128)(2,1)} %copy.25), calls=%async_computation | async-start | bytes 786432 | tf_op jit(solution)/shard_map/all_to_all | solution.py:14
  40.8 3.2 %collective-permute-start.5 = (bf16[96,2376]{1,0:T(8,128)(2,1)}, bf16[96,2376]{1,0:T(8,128)(2,1)}, u32[]{:S(2)}, u32[]{:S(2)}) collective-permute-start(bf16[96,2376]{1,0:T(8,128)(2,1)} %collective-permute-done.1), channel_id=1, source_target_pairs={{0,96},{32,0},{64,32},{96,64},{1,97},{33,1},{65,33},{97,65},{2,98}... | collective-permute-start | bytes 1368584 | tf_op jit(solution)/shard_map/ppermute | solution.py:83
  44.0 2.8 %collective-permute-done.3 = bf16[96,2376]{1,0:T(8,128)(2,1)} collective-permute-done((bf16[96,2376]{1,0:T(8,128)(2,1)S(1)}, bf16[96,2376]{1,0:T(8,128)(2,1)}, u32[]{:S(2)}, u32[]{:S(2)}) %collective-permute-start.3) | collective-permute-done | bytes 456224 | tf_op jit(solution)/shard_map/ppermute | solution.py:82
  47.8 2.2 collective-permute-start.6
  51.1 1.4 constant_dynamic-update-slice_fusion.2
  52.5 4.5 %all-to-all-done = bf16[6,4,32,192]{3,1,2,0:T(4,128)(2,1)S(1)} async-done(((bf16[6,4,32,192]{3,1,2,0:T(4,128)(2,1)}), bf16[6,4,32,192]{3,1,2,0:T(4,128)(2,1)S(1)}, u32[]{:S(2)}, u32[]{:S(2)}) %all-to-all-start) | async-done | bytes 294944 | tf_op jit(solution)/shard_map/all_to_all | solution.py:14
  59.9 2.5 collective-permute-done.6
  64.4 4.3 %collective-permute-start.7 = (f32[32,2376]{1,0:T(8,128)S(1)}, f32[32,2376]{1,0:T(8,128)S(1)}, u32[]{:S(2)}, u32[]{:S(2)}) collective-permute-start(f32[32,2376]{1,0:T(8,128)S(1)} %get-tuple-element.25), channel_id=1, source_target_pairs={{0,128},{1,129},{2,130},{3,131},{4,132},{5,133},{6,134},{7,135},{8... | collective-permute-start | bytes 912392 | tf_op jit(solution)/shard_map/ppermute | solution.py:43
  69.4 4.8 %collective-permute-done.7 = f32[32,2376]{1,0:T(8,128)S(1)} collective-permute-done((f32[32,2376]{1,0:T(8,128)S(1)}, f32[32,2376]{1,0:T(8,128)S(1)}, u32[]{:S(2)}, u32[]{:S(2)}) %collective-permute-start.7) | collective-permute-done | bytes 304160 | tf_op jit(solution)/shard_map/ppermute | solution.py:43
  75.0 4.4 %collective-permute-start.9 = (f32[32,2376]{1,0:T(8,128)S(1)}, f32[32,2376]{1,0:T(8,128)S(1)}, u32[]{:S(2)}, u32[]{:S(2)}) collective-permute-start(f32[32,2376]{1,0:T(8,128)S(1)} %get-tuple-element.27), channel_id=1, source_target_pairs={{0,128},{128,256},{1,129},{129,257},{2,130},{130,258},{3,131},{131... | collective-permute-start | bytes 912392 | tf_op jit(solution)/shard_map/ppermute | solution.py:43
  79.4 4.7 %collective-permute-done.9 = f32[32,2376]{1,0:T(8,128)S(1)} collective-permute-done((f32[32,2376]{1,0:T(8,128)S(1)}, f32[32,2376]{1,0:T(8,128)S(1)}, u32[]{:S(2)}, u32[]{:S(2)}) %collective-permute-start.9) | collective-permute-done | bytes 304160 | tf_op jit(solution)/shard_map/ppermute | solution.py:43
  84.1 4.4 %collective-permute-start.11 = (f32[32,2376]{1,0:T(8,128)S(1)}, f32[32,2376]{1,0:T(8,128)S(1)}, u32[]{:S(2)}, u32[]{:S(2)}) collective-permute-start(f32[32,2376]{1,0:T(8,128)S(1)} %get-tuple-element.29), channel_id=1, source_target_pairs={{0,128},{128,256},{256,384},{1,129},{129,257},{257,385},{2,130},{1... | collective-permute-start | bytes 912392 | tf_op jit(solution)/shard_map/ppermute | solution.py:43
  89.2 3.7 %collective-permute-done.11 = f32[32,2376]{1,0:T(8,128)S(1)} collective-permute-done((f32[32,2376]{1,0:T(8,128)S(1)}, f32[32,2376]{1,0:T(8,128)S(1)}, u32[]{:S(2)}, u32[]{:S(2)}) %collective-permute-start.11) | collective-permute-done | bytes 304160 | tf_op jit(solution)/shard_map/ppermute | solution.py:43
  93.7 5.1 %collective-permute-start.13 = (f32[32,2376]{1,0:T(8,128)}, f32[32,2376]{1,0:T(8,128)}, u32[]{:S(2)}, u32[]{:S(2)}) collective-permute-start(f32[32,2376]{1,0:T(8,128)} %get-tuple-element.31), channel_id=1, source_target_pairs={{0,128},{128,256},{256,384},{384,512},{1,129},{129,257},{257,385},... | collective-permute-start | bytes 912392 | tf_op jit(solution)/shard_map/ppermute | solution.py:43
  98.8 1.4 collective-permute-start.14
  100.3 2.5 collective-permute-done.13
  104.0 14.6 %collective-permute-start.15 = (f32[32,2376]{1,0:T(8,128)S(1)}, f32[32,2376]{1,0:T(8,128)S(1)}, u32[]{:S(2)}, u32[]{:S(2)}) collective-permute-start(f32[32,2376]{1,0:T(8,128)S(1)} %get-tuple-element.33), channel_id=1, source_target_pairs={{0,128},{128,256},{256,384},{384,512},{512,640},{1,129},{129,257},... | collective-permute-start | bytes 912392 | tf_op jit(solution)/shard_map/ppermute | solution.py:43
  120.0 3.0 %collective-permute-done.15 = f32[32,2376]{1,0:T(8,128)S(1)} collective-permute-done((f32[32,2376]{1,0:T(8,128)S(1)}, f32[32,2376]{1,0:T(8,128)S(1)}, u32[]{:S(2)}, u32[]{:S(2)}) %collective-permute-start.15) | collective-permute-done | bytes 304160 | tf_op jit(solution)/shard_map/ppermute | solution.py:43
  123.0 4.4 %collective-permute-done.16 = f32[32,2376]{1,0:T(8,128)S(1)} collective-permute-done((f32[32,2376]{1,0:T(8,128)S(1)}, f32[32,2376]{1,0:T(8,128)S(1)}, u32[]{:S(2)}, u32[]{:S(2)}) %collective-permute-start.16) | collective-permute-done | bytes 304160 | tf_op jit(solution)/shard_map/ppermute | solution.py:44
  128.7 2.5 collective-permute-start.17
  132.5 1.4 collective-permute-done.17
  134.0 5.1 %collective-permute-done.18 = bf16[32,2432]{1,0:T(8,128)(2,1)S(1)} collective-permute-done((bf16[32,2432]{1,0:T(8,128)(2,1)S(1)}, bf16[32,2432]{1,0:T(8,128)(2,1)S(1)}, u32[]{:S(2)}, u32[]{:S(2)}) %collective-permute-start.18) | collective-permute-done | bytes 155680 | tf_op jit(solution)/shard_map/ppermute | solution.py:52
  141.0 7.3 %collective-permute-done.20 = bf16[32,2432]{1,0:T(8,128)(2,1)S(1)} collective-permute-done((bf16[32,2432]{1,0:T(8,128)(2,1)S(1)}, bf16[32,2432]{1,0:T(8,128)(2,1)S(1)}, u32[]{:S(2)}, u32[]{:S(2)}) %collective-permute-start.20) | collective-permute-done | bytes 155680 | tf_op jit(solution)/shard_map/ppermute | solution.py:52
  151.0 7.2 %collective-permute-done.22 = bf16[32,2432]{1,0:T(8,128)(2,1)S(1)} collective-permute-done((bf16[32,2432]{1,0:T(8,128)(2,1)S(1)}, bf16[32,2432]{1,0:T(8,128)(2,1)S(1)}, u32[]{:S(2)}, u32[]{:S(2)}) %collective-permute-start.22) | collective-permute-done | bytes 155680 | tf_op jit(solution)/shard_map/ppermute | solution.py:52
  160.2 6.0 %collective-permute-done.24 = bf16[32,2432]{1,0:T(8,128)(2,1)S(1)} collective-permute-done((bf16[32,2432]{1,0:T(8,128)(2,1)S(1)}, bf16[32,2432]{1,0:T(8,128)(2,1)S(1)}, u32[]{:S(2)}, u32[]{:S(2)}) %collective-permute-start.24) | collective-permute-done | bytes 155680 | tf_op jit(solution)/shard_map/ppermute | solution.py:52
  168.5 5.7 %collective-permute-done.26 = bf16[32,2432]{1,0:T(8,128)(2,1)} collective-permute-done((bf16[32,2432]{1,0:T(8,128)(2,1)S(1)}, bf16[32,2432]{1,0:T(8,128)(2,1)}, u32[]{:S(2)}, u32[]{:S(2)}) %collective-permute-start.26) | collective-permute-done | bytes 155680 | tf_op jit(solution)/shard_map/ppermute | solution.py:52
  174.2 1.6 select_dynamic-update-slice_fusion.4
  179.7 1.7 fusion.11
  183.1 2.2 collective-permute-start.27
  185.6 5.5 %collective-permute-start.28 = (f32[192,256]{1,0:T(8,128)S(1)}, f32[192,256]{1,0:T(8,128)S(1)}, u32[]{:S(2)}, u32[]{:S(2)}) collective-permute-start(f32[192,256]{1,0:T(8,128)S(1)} %concatenate.142), channel_id=1, source_target_pairs={{0,64},{32,96},{64,0},{96,32},{1,65},{33,97},{65,1},{97,33},{2,66}... | collective-permute-start | bytes 589832 | tf_op jit(solution)/shard_map/ppermute | solution.py:131
  191.3 2.1 collective-permute-start.29
  193.4 1.6 fusion.13
  195.4 3.5 %collective-permute-done.29 = f32[192,256]{1,0:T(8,128)S(1)} collective-permute-done((f32[192,256]{1,0:T(8,128)S(1)}, f32[192,256]{1,0:T(8,128)S(1)}, u32[]{:S(2)}, u32[]{:S(2)}) %collective-permute-start.29) | collective-permute-done | bytes 196640 | tf_op jit(solution)/shard_map/ppermute | solution.py:131
  198.9 2.7 %gather_fusion.3 = f32[832,256]{1,0:T(8,128)S(1)} fusion(f32[768,256]{1,0:T(8,128)S(1)} %pad_maximum_fusion, s32[1024]{0:T(1024)S(1)} %pad_clamp_fusion.3), kind=kCustom, calls=%fused_computation.3 | custom fusion | bytes 1707264 | tf_op jit(solution)/shard_map/jit(_take)/gather | solution.py:140
  201.7 1.9 collective-permute-start.30
  204.4 18.3 %all-to-all-start.2 = ((bf16[16,24,192]{2,1,0:T(8,128)(2,1)}), bf16[16,24,192]{2,1,0:T(8,128)(2,1)S(1)}, u32[]{:S(2)}, u32[]{:S(2)}) async-start(bf16[16,24,192]{2,1,0:T(8,128)(2,1)} %bitcast.16), calls=%async_computation.2 | async-start | bytes 393216 | tf_op jit(solution)/shard_map/all_to_all | solution.py:14
  225.4 12.0 %all-to-all-done.2 = bf16[16,24,192]{2,1,0:T(8,128)(2,1)S(1)} async-done(((bf16[16,24,192]{2,1,0:T(8,128)(2,1)}), bf16[16,24,192]{2,1,0:T(8,128)(2,1)S(1)}, u32[]{:S(2)}, u32[]{:S(2)}) %all-to-all-start.2) | async-done | bytes 147488 | tf_op jit(solution)/shard_map/all_to_all | solution.py:14
  237.4 5.6 %all-to-all-start.1 = ((f32[16,32,192]{2,1,0:T(8,128)}), f32[16,32,192]{2,1,0:T(8,128)S(1)}, u32[]{:S(2)}, u32[]{:S(2)}) async-start(f32[16,32,192]{2,1,0:T(8,128)} %fusion.15), calls=%async_computation.1 | async-start | bytes 1048576 | tf_op jit(solution)/shard_map/all_to_all | solution.py:152
  245.2 19.4 %all-to-all-done.1 = f32[16,32,192]{2,1,0:T(8,128)S(1)} async-done(((f32[16,32,192]{2,1,0:T(8,128)}), f32[16,32,192]{2,1,0:T(8,128)S(1)}, u32[]{:S(2)}, u32[]{:S(2)}) %all-to-all-start.1) | async-done | bytes 393248 | tf_op jit(solution)/shard_map/all_to_all | solution.py:152
  (158 shorter events, 39.8 us)
Async XLA Ops:
  0.6 243.8 %copy-start = (f32[768]{0:T(1024)S(1)}, f32[768]{0:T(1024)}, u32[]{:S(2)}) copy-start(f32[768]{0:T(1024)} %param.9) | copy-start | bytes 9220
  0.6 4.6 %copy-start.1 = (s32[192]{0:T(256)S(1)}, s32[192]{0:T(256)}, u32[]{:S(2)}) copy-start(s32[192]{0:T(256)} %param.11) | copy-start | bytes 2308
  2.7 37.1 %collective-permute-start.1 = (bf16[96,2376]{1,0:T(8,128)(2,1)S(1)}, bf16[96,2376]{1,0:T(8,128)(2,1)}, u32[]{:S(2)}, u32[]{:S(2)}) collective-permute-start(bf16[96,2376]{1,0:T(8,128)(2,1)S(1)} %get-tuple-element.71), channel_id=1, source_target_pairs={{0,96},{32,0},{64,32},{96,64},{1,97},{33,1},{65,33},{97,65},{2,98}... | collective-permute-start | bytes 1368584 | tf_op jit(solution)/shard_map/ppermute | solution.py:81
  5.2 5.1 %copy-start.2 = (s32[768]{0:T(1024)S(1)}, s32[768]{0:T(1024)}, u32[]{:S(2)}) copy-start(s32[768]{0:T(1024)} %param.8) | copy-start | bytes 9220
  10.4 3.2 %copy-start.4 = (bf16[192,2376]{1,0:T(8,128)(2,1)S(1)}, bf16[192,2376]{1,0:T(8,128)(2,1)}, u32[]{:S(2)}) copy-start(bf16[192,2376]{1,0:T(8,128)(2,1)} %param.7) | copy-start | bytes 2737156
  13.6 12.7 %copy-start.11 = (bf16[32,4608]{1,0:T(8,128)(2,1)S(1)}, bf16[32,4608]{1,0:T(8,128)(2,1)}, u32[]{:S(2)}) copy-start(bf16[32,4608]{1,0:T(8,128)(2,1)} %param.6) | copy-start | bytes 884740
  15.1 24.6 %collective-permute-start = (bf16[384,192]{0,1:T(8,128)(2,1)S(1)}, bf16[384,192]{0,1:T(8,128)(2,1)S(1)}, u32[]{:S(2)}, u32[]{:S(2)}) collective-permute-start(bf16[384,192]{0,1:T(8,128)(2,1)S(1)} %slice.228), channel_id=1, source_target_pairs={{0,1},{1,0},{2,3},{3,2},{4,5},{5,4},{6,7},{7,6},{8,9},{9,8},{10,11... | collective-permute-start | bytes 442376 | tf_op jit(solution)/shard_map/ppermute | solution.py:101
  17.1 34.1 %collective-permute-start.2 = (bf16[96,2376]{1,0:T(8,128)(2,1)}, bf16[96,2376]{1,0:T(8,128)(2,1)}, u32[]{:S(2)}, u32[]{:S(2)}) collective-permute-start(bf16[96,2376]{1,0:T(8,128)(2,1)} %get-tuple-element.70), channel_id=1, source_target_pairs={{0,96},{32,0},{64,32},{96,64},{1,97},{33,1},{65,33},{97,65},{2,98}... | collective-permute-start | bytes 1368584 | tf_op jit(solution)/shard_map/ppermute | solution.py:82
  21.7 26.1 %collective-permute-start.4 = (bf16[96,2376]{1,0:T(8,128)(2,1)}, bf16[96,2376]{1,0:T(8,128)(2,1)}, u32[]{:S(2)}, u32[]{:S(2)}) collective-permute-start(bf16[96,2376]{1,0:T(8,128)(2,1)} %get-tuple-element.70), channel_id=1, source_target_pairs={{0,32},{32,64},{64,96},{96,0},{1,33},{33,65},{65,97},{97,1},{2,34}... | collective-permute-start | bytes 1368584 | tf_op jit(solution)/shard_map/ppermute | solution.py:81
  23.7 23.1 %collective-permute-start.3 = (bf16[96,2376]{1,0:T(8,128)(2,1)S(1)}, bf16[96,2376]{1,0:T(8,128)(2,1)}, u32[]{:S(2)}, u32[]{:S(2)}) collective-permute-start(bf16[96,2376]{1,0:T(8,128)(2,1)S(1)} %get-tuple-element.71), channel_id=1, source_target_pairs={{0,32},{32,64},{64,96},{96,0},{1,33},{33,65},{65,97},{97,1},{2,34}... | collective-permute-start | bytes 1368584 | tf_op jit(solution)/shard_map/ppermute | solution.py:82
  27.6 29.4 %all-to-all-start = ((bf16[6,4,32,192]{3,1,2,0:T(4,128)(2,1)}), bf16[6,4,32,192]{3,1,2,0:T(4,128)(2,1)S(1)}, u32[]{:S(2)}, u32[]{:S(2)}) async-start(bf16[6,4,32,192]{3,1,2,0:T(4,128)(2,1)} %copy.25), calls=%async_computation | async-start | bytes 786432 | tf_op jit(solution)/shard_map/all_to_all | solution.py:14
  40.8 18.0 %collective-permute-start.5 = (bf16[96,2376]{1,0:T(8,128)(2,1)}, bf16[96,2376]{1,0:T(8,128)(2,1)}, u32[]{:S(2)}, u32[]{:S(2)}) collective-permute-start(bf16[96,2376]{1,0:T(8,128)(2,1)} %collective-permute-done.1), channel_id=1, source_target_pairs={{0,96},{32,0},{64,32},{96,64},{1,97},{33,1},{65,33},{97,65},{2,98}... | collective-permute-start | bytes 1368584 | tf_op jit(solution)/shard_map/ppermute | solution.py:83
  47.8 14.5 %collective-permute-start.6 = (bf16[96,2376]{1,0:T(8,128)(2,1)}, bf16[96,2376]{1,0:T(8,128)(2,1)}, u32[]{:S(2)}, u32[]{:S(2)}) collective-permute-start(bf16[96,2376]{1,0:T(8,128)(2,1)} %collective-permute-done.4), channel_id=1, source_target_pairs={{0,32},{32,64},{64,96},{96,0},{1,33},{33,65},{65,97},{97,1},{2,34}... | collective-permute-start | bytes 1368584 | tf_op jit(solution)/shard_map/ppermute | solution.py:83
  51.1 7.2 %copy-start.7 = (bf16[192,2376]{1,0:T(8,128)(2,1)}, bf16[192,2376]{1,0:T(8,128)(2,1)S(1)}, u32[]{:S(2)}) copy-start(bf16[192,2376]{1,0:T(8,128)(2,1)S(1)} %constant_dynamic-update-slice_fusion.4) | copy-start | bytes 2737156
  52.5 5.4 %copy-start.5 = (bf16[192,2376]{1,0:T(8,128)(2,1)}, bf16[192,2376]{1,0:T(8,128)(2,1)S(1)}, u32[]{:S(2)}) copy-start(bf16[192,2376]{1,0:T(8,128)(2,1)S(1)} %constant_dynamic-update-slice_fusion.2) | copy-start | bytes 2737156
  63.4 0.9 copy-start.9
  64.4 9.8 %collective-permute-start.7 = (f32[32,2376]{1,0:T(8,128)S(1)}, f32[32,2376]{1,0:T(8,128)S(1)}, u32[]{:S(2)}, u32[]{:S(2)}) collective-permute-start(f32[32,2376]{1,0:T(8,128)S(1)} %get-tuple-element.25), channel_id=1, source_target_pairs={{0,128},{1,129},{2,130},{3,131},{4,132},{5,133},{6,134},{7,135},{8... | collective-permute-start | bytes 912392 | tf_op jit(solution)/shard_map/ppermute | solution.py:43
  68.7 5.5 %collective-permute-start.8 = (f32[32,2376]{1,0:T(8,128)S(1)}, f32[32,2376]{1,0:T(8,128)S(1)}, u32[]{:S(2)}, u32[]{:S(2)}) collective-permute-start(f32[32,2376]{1,0:T(8,128)S(1)} %get-tuple-element.26), channel_id=1, source_target_pairs={{640,512},{641,513},{642,514},{643,515},{644,516},{645,517},{646,5... | collective-permute-start | bytes 912392 | tf_op jit(solution)/shard_map/ppermute | solution.py:44
  74.3 5.1 %collective-permute-start.10 = (f32[32,2376]{1,0:T(8,128)S(1)}, f32[32,2376]{1,0:T(8,128)S(1)}, u32[]{:S(2)}, u32[]{:S(2)}) collective-permute-start(f32[32,2376]{1,0:T(8,128)S(1)} %get-tuple-element.28), channel_id=1, source_target_pairs={{512,384},{640,512},{513,385},{641,513},{514,386},{642,514},{515,3... | collective-permute-start | bytes 912392 | tf_op jit(solution)/shard_map/ppermute | solution.py:44
  75.0 9.1 %collective-permute-start.9 = (f32[32,2376]{1,0:T(8,128)S(1)}, f32[32,2376]{1,0:T(8,128)S(1)}, u32[]{:S(2)}, u32[]{:S(2)}) collective-permute-start(f32[32,2376]{1,0:T(8,128)S(1)} %get-tuple-element.27), channel_id=1, source_target_pairs={{0,128},{128,256},{1,129},{129,257},{2,130},{130,258},{3,131},{131... | collective-permute-start | bytes 912392 | tf_op jit(solution)/shard_map/ppermute | solution.py:43
  84.1 8.8 %collective-permute-start.11 = (f32[32,2376]{1,0:T(8,128)S(1)}, f32[32,2376]{1,0:T(8,128)S(1)}, u32[]{:S(2)}, u32[]{:S(2)}) collective-permute-start(f32[32,2376]{1,0:T(8,128)S(1)} %get-tuple-element.29), channel_id=1, source_target_pairs={{0,128},{128,256},{256,384},{1,129},{129,257},{257,385},{2,130},{1... | collective-permute-start | bytes 912392 | tf_op jit(solution)/shard_map/ppermute | solution.py:43
  88.5 4.4 %collective-permute-start.12 = (f32[32,2376]{1,0:T(8,128)S(1)}, f32[32,2376]{1,0:T(8,128)S(1)}, u32[]{:S(2)}, u32[]{:S(2)}) collective-permute-start(f32[32,2376]{1,0:T(8,128)S(1)} %get-tuple-element.30), channel_id=1, source_target_pairs={{384,256},{512,384},{640,512},{385,257},{513,385},{641,513},{386,2... | collective-permute-start | bytes 912392 | tf_op jit(solution)/shard_map/ppermute | solution.py:44
  93.7 9.1 %collective-permute-start.13 = (f32[32,2376]{1,0:T(8,128)}, f32[32,2376]{1,0:T(8,128)}, u32[]{:S(2)}, u32[]{:S(2)}) collective-permute-start(f32[32,2376]{1,0:T(8,128)} %get-tuple-element.31), channel_id=1, source_target_pairs={{0,128},{128,256},{256,384},{384,512},{1,129},{129,257},{257,385},... | collective-permute-start | bytes 912392 | tf_op jit(solution)/shard_map/ppermute | solution.py:43
  98.8 4.0 %collective-permute-start.14 = (f32[32,2376]{1,0:T(8,128)S(1)}, f32[32,2376]{1,0:T(8,128)}, u32[]{:S(2)}, u32[]{:S(2)}) collective-permute-start(f32[32,2376]{1,0:T(8,128)S(1)} %get-tuple-element.32), channel_id=1, source_target_pairs={{256,128},{384,256},{512,384},{640,512},{257,129},{385,257},{513,3... | collective-permute-start | bytes 912392 | tf_op jit(solution)/shard_map/ppermute | solution.py:44
  104.0 19.0 %collective-permute-start.15 = (f32[32,2376]{1,0:T(8,128)S(1)}, f32[32,2376]{1,0:T(8,128)S(1)}, u32[]{:S(2)}, u32[]{:S(2)}) collective-permute-start(f32[32,2376]{1,0:T(8,128)S(1)} %get-tuple-element.33), channel_id=1, source_target_pairs={{0,128},{128,256},{256,384},{384,512},{512,640},{1,129},{129,257},... | collective-permute-start | bytes 912392 | tf_op jit(solution)/shard_map/ppermute | solution.py:43
  118.7 8.8 %collective-permute-start.16 = (f32[32,2376]{1,0:T(8,128)S(1)}, f32[32,2376]{1,0:T(8,128)S(1)}, u32[]{:S(2)}, u32[]{:S(2)}) collective-permute-start(f32[32,2376]{1,0:T(8,128)S(1)} %get-tuple-element.34), channel_id=1, source_target_pairs={{128,0},{256,128},{384,256},{512,384},{640,512},{129,1},{257,129},... | collective-permute-start | bytes 912392 | tf_op jit(solution)/shard_map/ppermute | solution.py:44
  128.0 51.7 %copy-start.6 = (bf16[192,2376]{1,0:T(8,128)(2,1)S(1)}, bf16[192,2376]{1,0:T(8,128)(2,1)}, u32[]{:S(2)}) copy-start(bf16[192,2376]{1,0:T(8,128)(2,1)} %copy-done.5) | copy-start | bytes 2737156
  128.7 5.2 %collective-permute-start.17 = (bf16[32,2432]{1,0:T(8,128)(2,1)S(1)}, bf16[32,2432]{1,0:T(8,128)(2,1)S(1)}, u32[]{:S(2)}, u32[]{:S(2)}) collective-permute-start(bf16[32,2432]{1,0:T(8,128)(2,1)S(1)} %get-tuple-element.54), channel_id=1, source_target_pairs={{0,128},{128,256},{256,384},{384,512},{512,640},{1,129},{129,257},... | collective-permute-start | bytes 466952 | tf_op jit(solution)/shard_map/ppermute | solution.py:51
  131.2 7.8 %collective-permute-start.18 = (bf16[32,2432]{1,0:T(8,128)(2,1)S(1)}, bf16[32,2432]{1,0:T(8,128)(2,1)S(1)}, u32[]{:S(2)}, u32[]{:S(2)}) collective-permute-start(bf16[32,2432]{1,0:T(8,128)(2,1)S(1)} %get-tuple-element.54), channel_id=1, source_target_pairs={{128,0},{256,128},{384,256},{512,384},{640,512},{129,1},{257,129},... | collective-permute-start | bytes 466952 | tf_op jit(solution)/shard_map/ppermute | solution.py:52
  139.0 2.0 collective-permute-start.19
  139.7 8.6 %collective-permute-start.20 = (bf16[32,2432]{1,0:T(8,128)(2,1)S(1)}, bf16[32,2432]{1,0:T(8,128)(2,1)S(1)}, u32[]{:S(2)}, u32[]{:S(2)}) collective-permute-start(bf16[32,2432]{1,0:T(8,128)(2,1)S(1)} %collective-permute-done.18), channel_id=1, source_target_pairs={{128,0},{256,128},{384,256},{512,384},{129,1},{257,129},{385,257},... | collective-permute-start | bytes 466952 | tf_op jit(solution)/shard_map/ppermute | solution.py:52
  148.3 2.7 %collective-permute-start.21 = (bf16[32,2432]{1,0:T(8,128)(2,1)S(1)}, bf16[32,2432]{1,0:T(8,128)(2,1)S(1)}, u32[]{:S(2)}, u32[]{:S(2)}) collective-permute-start(bf16[32,2432]{1,0:T(8,128)(2,1)S(1)} %collective-permute-done.19), channel_id=1, source_target_pairs={{256,384},{384,512},{512,640},{257,385},{385,513},{513,641},{258,3... | collective-permute-start | bytes 466952 | tf_op jit(solution)/shard_map/ppermute | solution.py:51
  149.0 9.3 %collective-permute-start.22 = (bf16[32,2432]{1,0:T(8,128)(2,1)S(1)}, bf16[32,2432]{1,0:T(8,128)(2,1)S(1)}, u32[]{:S(2)}, u32[]{:S(2)}) collective-permute-start(bf16[32,2432]{1,0:T(8,128)(2,1)S(1)} %collective-permute-done.20), channel_id=1, source_target_pairs={{128,0},{256,128},{384,256},{129,1},{257,129},{385,257},{130,2},{2... | collective-permute-start | bytes 466952 | tf_op jit(solution)/shard_map/ppermute | solution.py:52
  158.3 2.0 collective-permute-start.23
  158.9 7.4 %collective-permute-start.24 = (bf16[32,2432]{1,0:T(8,128)(2,1)S(1)}, bf16[32,2432]{1,0:T(8,128)(2,1)S(1)}, u32[]{:S(2)}, u32[]{:S(2)}) collective-permute-start(bf16[32,2432]{1,0:T(8,128)(2,1)S(1)} %collective-permute-done.22), channel_id=1, source_target_pairs={{128,0},{256,128},{129,1},{257,129},{130,2},{258,130},{131,3},{259... | collective-permute-start | bytes 466952 | tf_op jit(solution)/shard_map/ppermute | solution.py:52
  166.3 2.2 collective-permute-start.25
  167.0 7.2 %collective-permute-start.26 = (bf16[32,2432]{1,0:T(8,128)(2,1)S(1)}, bf16[32,2432]{1,0:T(8,128)(2,1)}, u32[]{:S(2)}, u32[]{:S(2)}) collective-permute-start(bf16[32,2432]{1,0:T(8,128)(2,1)S(1)} %collective-permute-done.24), channel_id=1, source_target_pairs={{128,0},{129,1},{130,2},{131,3},{132,4},{133,5},{134,6},{135,7},{1... | collective-permute-start | bytes 466952 | tf_op jit(solution)/shard_map/ppermute | solution.py:52
  177.2 4.2 %copy-start.10 = (bf16[192,2376]{1,0:T(8,128)(2,1)S(1)}, bf16[192,2376]{1,0:T(8,128)(2,1)}, u32[]{:S(2)}) copy-start(bf16[192,2376]{1,0:T(8,128)(2,1)} %copy-done.9) | copy-start | bytes 2737156
  178.6 2.8 %copy-start.12 = (bf16[192,2432]{1,0:T(8,128)(2,1)S(1)}, bf16[192,2432]{1,0:T(8,128)(2,1)}, u32[]{:S(2)}) copy-start(bf16[192,2432]{1,0:T(8,128)(2,1)} %select_dynamic-update-slice_fusion) | copy-start | bytes 2801668
  179.7 2.2 copy-start.8
  183.1 12.3 %collective-permute-start.27 = (f32[192,256]{1,0:T(8,128)S(1)}, f32[192,256]{1,0:T(8,128)S(1)}, u32[]{:S(2)}, u32[]{:S(2)}) collective-permute-start(f32[192,256]{1,0:T(8,128)S(1)} %concatenate.141), channel_id=1, source_target_pairs={{0,32},{32,64},{64,96},{96,0},{1,33},{33,65},{65,97},{97,1},{2,34}... | collective-permute-start | bytes 589832 | tf_op jit(solution)/shard_map/ppermute | solution.py:131
  185.6 9.8 %collective-permute-start.28 = (f32[192,256]{1,0:T(8,128)S(1)}, f32[192,256]{1,0:T(8,128)S(1)}, u32[]{:S(2)}, u32[]{:S(2)}) collective-permute-start(f32[192,256]{1,0:T(8,128)S(1)} %concatenate.142), channel_id=1, source_target_pairs={{0,64},{32,96},{64,0},{96,32},{1,65},{33,97},{65,1},{97,33},{2,66}... | collective-permute-start | bytes 589832 | tf_op jit(solution)/shard_map/ppermute | solution.py:131
  191.3 7.6 %collective-permute-start.29 = (f32[192,256]{1,0:T(8,128)S(1)}, f32[192,256]{1,0:T(8,128)S(1)}, u32[]{:S(2)}, u32[]{:S(2)}) collective-permute-start(f32[192,256]{1,0:T(8,128)S(1)} %concatenate.143), channel_id=1, source_target_pairs={{0,96},{32,0},{64,32},{96,64},{1,97},{33,1},{65,33},{97,65},{2,98}... | collective-permute-start | bytes 589832 | tf_op jit(solution)/shard_map/ppermute | solution.py:131
  201.7 21.1 %collective-permute-start.30 = (f32[416,256]{1,0:T(8,128)S(1)}, f32[416,256]{1,0:T(8,128)S(1)}, u32[]{:S(2)}, u32[]{:S(2)}) collective-permute-start(f32[416,256]{1,0:T(8,128)S(1)} %slice.249), channel_id=1, source_target_pairs={{0,1},{1,0},{2,3},{3,2},{4,5},{5,4},{6,7},{7,6},{8,9},{9,8},{10,11... | collective-permute-start | bytes 1277960 | tf_op jit(solution)/shard_map/ppermute | solution.py:143
  204.4 32.9 %all-to-all-start.2 = ((bf16[16,24,192]{2,1,0:T(8,128)(2,1)}), bf16[16,24,192]{2,1,0:T(8,128)(2,1)S(1)}, u32[]{:S(2)}, u32[]{:S(2)}) async-start(bf16[16,24,192]{2,1,0:T(8,128)(2,1)} %bitcast.16), calls=%async_computation.2 | async-start | bytes 393216 | tf_op jit(solution)/shard_map/all_to_all | solution.py:14
  223.5 20.3 %copy-start.3 = (s32[192]{0:T(256)S(1)}, s32[192]{0:T(256)}, u32[]{:S(2)}) copy-start(s32[192]{0:T(256)} %param.10) | copy-start | bytes 2308
  237.4 27.2 %all-to-all-start.1 = ((f32[16,32,192]{2,1,0:T(8,128)}), f32[16,32,192]{2,1,0:T(8,128)S(1)}, u32[]{:S(2)}, u32[]{:S(2)}) async-start(f32[16,32,192]{2,1,0:T(8,128)} %fusion.15), calls=%async_computation.1 | async-start | bytes 1048576 | tf_op jit(solution)/shard_map/all_to_all | solution.py:152

commit v3 on v2

v3 whole, which is shorter than its diff:
```python
import jax
import jax.numpy as jnp
from jax import lax
from jax.sharding import Mesh, PartitionSpec as P

BLK = 4
NA, NB, NX, NY, NH, NC = 3, 2, 4, 8, 2, 2
NZ = NA * NB
VOC = ("y", "zh", "c")
LINE = ("za", "zb")
NV = NY * NH * NC
F32, BF16 = jnp.float32, jnp.bfloat16


def trade(a, axes):
    return lax.all_to_all(a, axes, split_axis=0, concat_axis=0, tiled=True)


def roll_to(a, axis, start):
    return lax.dynamic_slice_in_dim(jnp.concatenate([a, a], axis), start, a.shape[axis], axis)


def stat_lanes(stats, lanes):
    lane = lax.broadcasted_iota(jnp.int32, (stats[0].shape[0], lanes), 1)
    value = jnp.zeros(lane.shape, F32)
    for k, a in enumerate(stats):
        value = jnp.where(lane // 3 == k, a[:, None], value)
    hi = lax.reduce_precision(value, 8, 7)
    rest = value - hi
    mid = lax.reduce_precision(rest, 8, 7)
    return jnp.where(lane % 3 == 0, hi, jnp.where(lane % 3 == 1, mid, rest - mid)).astype(BF16)


def join3(cols):
    cols = cols.astype(F32)
    return (cols[:, 0] + cols[:, 1]) + cols[:, 2]


def merge(a, b, feats):
    top = jnp.maximum(a[:, feats], b[:, feats])[:, None]
    fa, fb = jnp.exp(a[:, feats : feats + 1] - top), jnp.exp(b[:, feats : feats + 1] - top)
    summed = fa * a + fb * b
    goal = a[:, feats + 2] + b[:, feats + 2]
    return summed[:, :feats], top[:, 0], summed[:, feats + 1], goal


def body(hidden, weight, targets, advantage, counts, block_order):
    per, _ = hidden.shape
    feats, width = weight.shape
    rows = targets.shape[0]
    z, x, core = lax.axis_index(LINE), lax.axis_index("x"), lax.axis_index("c")
    v = lax.axis_index(VOC)
    share = rows // NV
    back = [(i, (i - 1) % NX) for i in range(NX)]
    forth = [(i, (i + 1) % NX) for i in range(NX)]
    swap = [(0, 1), (1, 0)]

    half = feats // 2
    up, down = weight[:half], weight[half:]
    u1, d3 = lax.ppermute(up, "x", back), lax.ppermute(down, "x", forth)
    d1, u3 = lax.ppermute(down, "x", back), lax.ppermute(up, "x", forth)
    u2, d2 = lax.ppermute(u1, "x", back), lax.ppermute(d3, "x", forth)
    w = [(0, 0, up), (0, half, down), (1, 0, u1), (1, half, d1)]
    w += [(3, 0, u3), (3, half, d3), (2, 0, u2), (2, half, d2)]

    h = hidden.reshape(per, NZ, NX * 2, half).transpose(1, 2, 0, 3)
    h = trade(h, LINE).reshape(NA, NB, NX, 2, per, half).transpose(1, 2, 3, 0, 4, 5)
    h = roll_to(roll_to(h, 1, x), 0, 1 - lax.axis_index("zb"))

    k = jnp.arange(rows // NC, dtype=jnp.int32)
    pair = (k // share) * (NC * share) + k % share
    position = jnp.concatenate([pair + (1 - core) * share, pair + core * share])
    blocks = block_order[position // BLK]
    source = blocks * BLK + position % BLK
    wanted = targets[source]

    columns = v * width + jnp.arange(width, dtype=jnp.int32)
    onehot = (wanted[:, None] == columns[None, :]).astype(BF16)
    picked = lax.dot_general(
        onehot, weight, (((1,), (1,)), ((), ())), preferred_element_type=F32
    ).astype(BF16)
    picked = picked[rows // NC :] + lax.ppermute(picked[: rows // NC], "c", swap)

    parts = []
    for r in range(NB):
        part = None
        for o, first, rows_w in w:
            d = jnp.dot(
                h[r, o, first // half].reshape(NA * per, half), rows_w, preferred_element_type=F32
            )
            part = d if part is None else part + d
        parts.append(part)
    logits = parts[1] + lax.ppermute(parts[0], "zb", swap)
    logits = jnp.sum(trade(logits.reshape(NA, per, width), "za"), axis=0)

    mine = lax.dynamic_slice_in_dim(targets, (z * NX + x) * per, per, 0)
    top = jnp.max(logits, axis=1)
    e = jnp.exp(logits - top[:, None])
    total = jnp.sum(e, axis=1)
    hit = mine[:, None] == columns[None, :]
    goal = jnp.sum(jnp.where(hit, logits, F32(0.0)), axis=1)

    lanes = -(-width // 128) * 128
    sent = jnp.concatenate(
        [e.astype(BF16), stat_lanes((top, total, goal), lanes - width)], 1
    )
    got = trade(jnp.broadcast_to(sent[None], (NZ, per, lanes)), LINE)
    got = got.reshape(NZ * per, lanes)
    probs = got[:, :width]
    stats = [join3(got[:, width + 3 * k : width + 3 * k + 3]) for k in range(3)]
    stats = jnp.stack(stats + [jnp.zeros_like(stats[0])] * (64 - 3), axis=1)

    pieces = [None] * NX
    for o in (2, 1, 3, 0):
        g = [
            lax.dot_general(probs, m, (((1,), (1,)), ((), ())), preferred_element_type=F32)
            for p, _, m in w
            if p == o
        ]
        g = jnp.concatenate(g + [stats], axis=1)
        pieces[o] = lax.ppermute(g, "x", [(i, (i + o) % NX) for i in range(NX)]) if o else g
    grads = jnp.concatenate(pieces, 0)

    here = (z * NX + x) * per
    own = here + jnp.arange(per, dtype=jnp.int32)
    own = block_order[own // BLK] * BLK + own % BLK
    order = jnp.concatenate([source[: rows // NC], own, source[rows // NC :], own])
    owner = order // per
    place = ((x - owner % NX) % NX) * (NZ * per) + (owner // NX) * per + order % per
    grads = jnp.take(grads, place, axis=0, mode="clip")
    cut = rows // NC + per
    grads, top, total, goal = merge(
        grads[cut:], lax.ppermute(grads[:cut], "c", swap), feats
    )
    kept, wide = rows // NC, NH * share
    lines = [a[:kept].reshape(NY, 1, wide) for a in (top, total)]
    lines += [jnp.broadcast_to(a[kept:].reshape(1, 1, per), (NY, 1, per)) for a in (top, total, goal)]
    lines = [jnp.pad(a, ((0, 0), (0, 0), (0, feats - a.shape[2]))) for a in lines]
    lines.append(jnp.zeros((NY, 3, feats), F32))
    blocks_of = [a.reshape(NY, wide, feats) for a in (grads[:kept], picked.astype(F32))]
    msg = trade(jnp.concatenate(blocks_of + lines, axis=1), "y")

    def over(tops, totals):
        peak = jnp.max(tops, axis=0)
        scale = jnp.exp(tops - peak[None])
        return scale, peak, jnp.sum(scale * totals, axis=0)

    base = 2 * wide
    scale, top, total = over(msg[:, base, :wide], msg[:, base + 1, :wide])
    mixed = jnp.sum(scale[:, :, None] * msg[:, :wide], axis=0)
    target_w = jnp.sum(msg[:, wide:base], axis=0)
    _, row_top, row_total = over(msg[:, base + 2, :per], msg[:, base + 3, :per])
    row_goal = jnp.sum(msg[:, base + 4, :per], axis=0)

    def half_of(side):
        pick = lambda a: lax.dynamic_index_in_dim(a.reshape((NH, share) + a.shape[1:]), side, 0, False)
        lines = [pick(top), pick(total), row_top, row_total, row_goal]
        lines = [jnp.pad(a, (0, feats - a.shape[0]))[None] for a in lines]
        return jnp.concatenate([pick(mixed), pick(target_w)] + lines + [jnp.zeros((3, feats), F32)], 0)

    zh = lax.axis_index("zh")
    far = lax.ppermute(half_of(1 - zh), "zh", swap)
    both = jnp.stack([half_of(zh), far])

    spot = v * share + jnp.arange(share, dtype=jnp.int32)
    block = block_order[spot // BLK]
    alive = spot % BLK < counts[block]
    coef = jnp.where(alive, advantage[block * BLK + spot % BLK], F32(0.0))

    base = 2 * share
    scale, _, norm = over(both[:, base, :share], both[:, base + 1, :share])
    mixed = jnp.sum(scale[:, :, None] * both[:, :share], axis=0) / norm[:, None]
    hidden_grad = coef[:, None] * (mixed - jnp.sum(both[:, share:base], axis=0))
    _, peak, norm = over(both[:, base + 2, :per], both[:, base + 3, :per])
    logprob = jnp.sum(both[:, base + 4, :per], axis=0) - (peak + jnp.log(norm))
    return (logprob, hidden_grad.astype(BF16))


def solution(mesh):
    fine = Mesh(mesh.devices.reshape(NA, NB, NX, NY, NH, NC), LINE + ("x",) + VOC)
    dp = LINE + ("x",)
    placed = (P(dp, None), P(dp, VOC), P(), P(), P(), P())

    return jax.shard_map(
        body, mesh=fine, in_specs=placed, out_specs=(P(dp), P(VOC, dp)), check_vma=False
    )
```

time: 268 us -> 247 us (0.922)
  the two profiles are of different devices: /device:TPU:10 before, /device:TPU:1 now
where the time goes in v3:
time: 247 us; the launch traced here: 246 us
  waiting for transfers between devices  108 us (44%)
  starting transfers between devices  81.3 us (33%)
  local copies, waits for them, and re-layouts  28.9 us (12%)
  matrix products  20.1 us (8%)
  other arithmetic  6.05 us (2%)
    all_to_all x4, waiting for transfers between devices, trade(): return lax.all_to_all(a, axes, split_axis=0, concat_axis=0, tiled=True)  74.1 us
    all_to_all x4, starting transfers between devices, trade(): return lax.all_to_all(a, axes, split_axis=0, concat_axis=0, tiled=True)  32.6 us
    ppermute x1, waiting for transfers between devices, body(): logits = parts[1] + lax.ppermute(parts[0], 'zb', swap)  16.8 us
    ppermute x3, starting transfers between devices, body(): lax.ppermute(g, 'x', [(i, (i + o) % NX) for i in range(NX)])  10.5 us
    ppermute x1, starting transfers between devices, body(): far = lax.ppermute(half_of(1 - zh), 'zh', swap)  9.75 us
    dot_general x16, matrix products, body(): jnp.dot(h[r, o, first // half].reshape(NA * per, half), rows_w, preferred...  9.42 us
    dot_general x8, matrix products, body(): lax.dot_general(probs, m, (((1,), (1,)), ((), ())), preferred_element_typ...  9.2 us
    ppermute x2, waiting for transfers between devices, body(): u2, d2 = (lax.ppermute(u1, 'x', back), lax.ppermute(d3, 'x', forth))  7.09 us
  transfers between devices with their start and end apart: 17, of which 11 were waited for; matrix products, arithmetic and copies ran while one was open for 13% of the time, Pallas kernels for 0%

profile of v3, /device:TPU:1, one launch (start us, length us, event | category | flops | bytes accessed | tf_op | source)
XLA Modules:
  0.0 246.2 jit_solution(3016212410793805966)
XLA Ops:
  0.6 1.3 reshape.840
  2.8 12.6 %all-to-all-start = ((bf16[6,8,32,96]{3,1,2,0:T(8,128)(2,1)}), bf16[6,8,32,96]{3,1,2,0:T(8,128)(2,1)S(1)}, u32[]{:S(2)}, u32[]{:S(2)}) async-start(bf16[6,8,32,96]{3,1,2,0:T(8,128)(2,1)} %copy.56), calls=%async_computation | async-start | bytes 786432 | tf_op jit(solution)/shard_map/all_to_all | solution.py:16
  15.5 1.0 fusion.98
  16.5 3.1 %collective-permute-start.3 = (bf16[96,2376]{1,0:T(8,128)(2,1)}, bf16[96,2376]{1,0:T(8,128)(2,1)S(1)}, u32[]{:S(2)}, u32[]{:S(2)}) collective-permute-start(bf16[96,2376]{1,0:T(8,128)(2,1)} %get-tuple-element.24), channel_id=1, source_target_pairs={{0,32},{32,64},{64,96},{96,0},{1,33},{33,65},{65,97},{97,1},{2,34}... | collective-permute-start | bytes 1368584 | tf_op jit(solution)/shard_map/ppermute | solution.py:60
  19.6 3.4 %collective-permute-start = (bf16[96,2376]{1,0:T(8,128)(2,1)}, bf16[96,2376]{1,0:T(8,128)(2,1)S(1)}, u32[]{:S(2)}, u32[]{:S(2)}) collective-permute-start(bf16[96,2376]{1,0:T(8,128)(2,1)} %get-tuple-element.25), channel_id=1, source_target_pairs={{0,96},{32,0},{64,32},{96,64},{1,97},{33,1},{65,33},{97,65},{2,98}... | collective-permute-start | bytes 1368584 | tf_op jit(solution)/shard_map/ppermute | solution.py:60
  23.0 3.2 %collective-permute-start.1 = (bf16[96,2376]{1,0:T(8,128)(2,1)}, bf16[96,2376]{1,0:T(8,128)(2,1)S(1)}, u32[]{:S(2)}, u32[]{:S(2)}) collective-permute-start(bf16[96,2376]{1,0:T(8,128)(2,1)} %get-tuple-element.24), channel_id=1, source_target_pairs={{0,96},{32,0},{64,32},{96,64},{1,97},{33,1},{65,33},{97,65},{2,98}... | collective-permute-start | bytes 1368584 | tf_op jit(solution)/shard_map/ppermute | solution.py:61
  26.2 2.1 collective-permute-start.2
  28.3 2.4 collective-permute-done.3
  30.7 2.3 collective-permute-start.5
  33.0 4.2 %collective-permute-start.4 = (bf16[96,2376]{1,0:T(8,128)(2,1)S(1)}, bf16[96,2376]{1,0:T(8,128)(2,1)}, u32[]{:S(2)}, u32[]{:S(2)}) collective-permute-start(bf16[96,2376]{1,0:T(8,128)(2,1)S(1)} %collective-permute-done), channel_id=1, source_target_pairs={{0,96},{32,0},{64,32},{96,64},{1,97},{33,1},{65,33},{97,65},{2,98}... | collective-permute-start | bytes 1368584 | tf_op jit(solution)/shard_map/ppermute | solution.py:62
  38.6 4.1 %collective-permute-done.1 = bf16[96,2376]{1,0:T(8,128)(2,1)S(1)} collective-permute-done((bf16[96,2376]{1,0:T(8,128)(2,1)}, bf16[96,2376]{1,0:T(8,128)(2,1)S(1)}, u32[]{:S(2)}, u32[]{:S(2)}) %collective-permute-start.1) | collective-permute-done | bytes 456224 | tf_op jit(solution)/shard_map/ppermute | solution.py:61
  44.4 6.2 %collective-permute-done.5 = bf16[96,2376]{1,0:T(8,128)(2,1)} collective-permute-done((bf16[96,2376]{1,0:T(8,128)(2,1)S(1)}, bf16[96,2376]{1,0:T(8,128)(2,1)}, u32[]{:S(2)}, u32[]{:S(2)}) %collective-permute-start.5) | collective-permute-done | bytes 456224 | tf_op jit(solution)/shard_map/ppermute | solution.py:62
  50.7 1.3 fusion.109
  52.8 1.3 fusion.12
  54.1 3.1 %collective-permute-start.6 = (f32[96,2376]{1,0:T(8,128)S(1)}, f32[96,2376]{1,0:T(8,128)S(1)}, u32[]{:S(2)}, u32[]{:S(2)}) collective-permute-start(f32[96,2376]{1,0:T(8,128)S(1)} %fusion.12), channel_id=1, source_target_pairs={{0,128},{128,0},{1,129},{129,1},{2,130},{130,2},{3,131},{131,3},{4... | collective-permute-start | bytes 2737160 | tf_op jit(solution)/shard_map/ppermute | solution.py:93
  58.1 1.3 fusion.105
  59.4 16.8 %collective-permute-done.6 = f32[96,2376]{1,0:T(8,128)S(1)} collective-permute-done((f32[96,2376]{1,0:T(8,128)S(1)}, f32[96,2376]{1,0:T(8,128)S(1)}, u32[]{:S(2)}, u32[]{:S(2)}) %collective-permute-start.6) | collective-permute-done | bytes 912416 | tf_op jit(solution)/shard_map/ppermute | solution.py:93
  76.2 2.2 fusion.8
  78.4 6.2 %all-to-all-start.1 = ((f32[3,32,2376]{2,1,0:T(8,128)}), f32[3,32,2376]{2,1,0:T(8,128)S(1)}, u32[]{:S(2)}, u32[]{:S(2)}) async-start(f32[3,32,2376]{2,1,0:T(8,128)} %bitcast.19), calls=%async_computation.1 | async-start | bytes 1867776 | tf_op jit(solution)/shard_map/all_to_all | solution.py:16
  84.8 29.4 %all-to-all-done.1 = f32[3,32,2376]{2,1,0:T(8,128)S(1)} async-done(((f32[3,32,2376]{2,1,0:T(8,128)}), f32[3,32,2376]{2,1,0:T(8,128)S(1)}, u32[]{:S(2)}, u32[]{:S(2)}) %all-to-all-start.1) | async-done | bytes 912416 | tf_op jit(solution)/shard_map/all_to_all | solution.py:16
  114.8 1.0 broadcast_in_dim.55
  115.8 6.2 %all-to-all-start.2 = ((bf16[6,32,2432]{2,1,0:T(8,128)(2,1)}), bf16[6,32,2432]{2,1,0:T(8,128)(2,1)S(1)}, u32[]{:S(2)}, u32[]{:S(2)}) async-start(bf16[6,32,2432]{2,1,0:T(8,128)(2,1)} %broadcast_in_dim.55), calls=%async_computation.2 | async-start | bytes 1867776 | tf_op jit(solution)/shard_map/all_to_all | solution.py:16
  122.1 5.0 %gather_fusion = s32[768]{0:T(1024)S(1)} fusion(s32[192]{0:T(256)S(1)} %copy-done.1, s32[1024]{0:T(1024)S(1)} %pad_clamp_fusion.6), kind=kCustom, calls=%fused_computation | custom fusion | bytes 9216 | tf_op jit(solution)/shard_map/gather | solution.py:73
  127.9 3.2 %gather_fusion.3 = s32[768]{0:T(1024)S(1)} fusion(s32[768]{0:T(1024)S(1)} %copy-done.2, s32[1024]{0:T(1024)S(1)} %pad_clamp_fusion.3), kind=kCustom, calls=%fused_computation.3 | custom fusion | bytes 9216 | tf_op jit(solution)/shard_map/gather | solution.py:75
  131.3 23.2 %all-to-all-done.2 = bf16[6,32,2432]{2,1,0:T(8,128)(2,1)S(1)} async-done(((bf16[6,32,2432]{2,1,0:T(8,128)(2,1)}), bf16[6,32,2432]{2,1,0:T(8,128)(2,1)S(1)}, u32[]{:S(2)}, u32[]{:S(2)}) %all-to-all-start.2) | async-done | bytes 933920 | tf_op jit(solution)/shard_map/all_to_all | solution.py:16
  156.1 1.1 fusion.30
  157.2 1.0 fusion.32
  158.3 1.9 concatenate.128
  160.2 3.1 %collective-permute-start.7 = (f32[192,256]{1,0:T(8,128)}, f32[192,256]{1,0:T(8,128)S(1)}, u32[]{:S(2)}, u32[]{:S(2)}) collective-permute-start(f32[192,256]{1,0:T(8,128)} %concatenate.128), channel_id=1, source_target_pairs={{0,32},{32,64},{64,96},{96,0},{1,33},{33,65},{65,97},{97,1},{2,34}... | collective-permute-start | bytes 589832 | tf_op jit(solution)/shard_map/ppermute | solution.py:121
  163.3 2.1 fusion.26
  165.4 2.1 fusion.28
  167.5 1.9 concatenate.129
  169.4 4.1 %collective-permute-start.8 = (f32[192,256]{1,0:T(8,128)}, f32[192,256]{1,0:T(8,128)}, u32[]{:S(2)}, u32[]{:S(2)}) collective-permute-start(f32[192,256]{1,0:T(8,128)} %concatenate.129), channel_id=1, source_target_pairs={{0,64},{32,96},{64,0},{96,32},{1,65},{33,97},{65,1},{97,33},{2,66}... | collective-permute-start | bytes 589832 | tf_op jit(solution)/shard_map/ppermute | solution.py:121
  173.5 1.1 fusion.22
  176.4 3.4 %collective-permute-start.9 = (f32[192,256]{1,0:T(8,128)}, f32[192,256]{1,0:T(8,128)S(1)}, u32[]{:S(2)}, u32[]{:S(2)}) collective-permute-start(f32[192,256]{1,0:T(8,128)} %concatenate.130), channel_id=1, source_target_pairs={{0,96},{32,0},{64,32},{96,64},{1,97},{33,1},{65,33},{97,65},{2,98}... | collective-permute-start | bytes 589832 | tf_op jit(solution)/shard_map/ppermute | solution.py:121
  179.7 1.1 fusion.36
  180.8 1.2 concatenate.127
  183.0 1.0 pad_maximum_fusion
  184.0 2.7 %gather_fusion.2 = f32[832,256]{1,0:T(8,128)S(1)} fusion(f32[768,256]{1,0:T(8,128)S(1)} %pad_maximum_fusion, s32[1024]{0:T(1024)S(1)} %pad_clamp_fusion.4), kind=kCustom, calls=%fused_computation.2 | custom fusion | bytes 1707264 | tf_op jit(solution)/shard_map/jit(_take)/gather | solution.py:130
  186.7 5.1 %collective-permute-start.10 = (f32[416,256]{1,0:T(8,128)S(1)}, f32[416,256]{1,0:T(8,128)S(1)}, u32[]{:S(2)}, u32[]{:S(2)}) collective-permute-start(f32[416,256]{1,0:T(8,128)S(1)} %slice.308), channel_id=1, source_target_pairs={{0,1},{1,0},{2,3},{3,2},{4,5},{5,4},{6,7},{7,6},{8,9},{9,8},{10,11... | collective-permute-start | bytes 1277960 | tf_op jit(solution)/shard_map/ppermute | solution.py:133
  191.8 1.5 fusion.13
  193.3 1.9 collective-permute-start.11
  195.3 1.3 collective-permute-done.11
  198.9 1.2 copy.61
  200.1 7.6 %all-to-all-start.3 = ((f32[8,104,192]{1,2,0:T(8,128)}), f32[8,104,192]{1,2,0:T(8,128)S(1)}, u32[]{:S(2)}, u32[]{:S(2)}) async-start(f32[8,104,192]{1,2,0:T(8,128)} %copy.61), calls=%async_computation.3 | async-start | bytes 1572864 | tf_op jit(solution)/shard_map/all_to_all | solution.py:16
  209.8 21.5 %all-to-all-done.3 = f32[8,104,192]{1,2,0:T(8,128)S(1)} async-done(((f32[8,104,192]{1,2,0:T(8,128)}), f32[8,104,192]{1,2,0:T(8,128)S(1)}, u32[]{:S(2)}, u32[]{:S(2)}) %all-to-all-start.3) | async-done | bytes 639008 | tf_op jit(solution)/shard_map/all_to_all | solution.py:16
  233.1 9.8 %collective-permute-start.12 = (f32[56,192]{1,0:T(8,128)S(1)}, f32[56,192]{1,0:T(8,128)S(1)}, u32[]{:S(2)}, u32[]{:S(2)}) collective-permute-start(f32[56,192]{1,0:T(8,128)S(1)} %concatenate.142), channel_id=1, source_target_pairs={{0,2},{2,0},{1,3},{3,1},{4,6},{6,4},{5,7},{7,5},{8,10},{10,8},{9,1... | collective-permute-start | bytes 129032 | tf_op jit(solution)/shard_map/ppermute | solution.py:162
  243.0 1.5 collective-permute-done.12
  (153 shorter events, 19.5 us)
Async XLA Ops:
  0.6 208.5 %copy-start = (f32[768]{0:T(1024)S(1)}, f32[768]{0:T(1024)}, u32[]{:S(2)}) copy-start(f32[768]{0:T(1024)} %param.9) | copy-start | bytes 9220
  2.0 13.5 %copy-start.4 = (bf16[192,2376]{1,0:T(8,128)(2,1)S(1)}, bf16[192,2376]{1,0:T(8,128)(2,1)}, u32[]{:S(2)}) copy-start(bf16[192,2376]{1,0:T(8,128)(2,1)} %param.7) | copy-start | bytes 2737156
  2.8 34.4 %all-to-all-start = ((bf16[6,8,32,96]{3,1,2,0:T(8,128)(2,1)}), bf16[6,8,32,96]{3,1,2,0:T(8,128)(2,1)S(1)}, u32[]{:S(2)}, u32[]{:S(2)}) async-start(bf16[6,8,32,96]{3,1,2,0:T(8,128)(2,1)} %copy.56), calls=%async_computation | async-start | bytes 786432 | tf_op jit(solution)/shard_map/all_to_all | solution.py:16
  16.5 14.2 %collective-permute-start.3 = (bf16[96,2376]{1,0:T(8,128)(2,1)}, bf16[96,2376]{1,0:T(8,128)(2,1)S(1)}, u32[]{:S(2)}, u32[]{:S(2)}) collective-permute-start(bf16[96,2376]{1,0:T(8,128)(2,1)} %get-tuple-element.24), channel_id=1, source_target_pairs={{0,32},{32,64},{64,96},{96,0},{1,33},{33,65},{65,97},{97,1},{2,34}... | collective-permute-start | bytes 1368584 | tf_op jit(solution)/shard_map/ppermute | solution.py:60
  19.6 13.4 %collective-permute-start = (bf16[96,2376]{1,0:T(8,128)(2,1)}, bf16[96,2376]{1,0:T(8,128)(2,1)S(1)}, u32[]{:S(2)}, u32[]{:S(2)}) collective-permute-start(bf16[96,2376]{1,0:T(8,128)(2,1)} %get-tuple-element.25), channel_id=1, source_target_pairs={{0,96},{32,0},{64,32},{96,64},{1,97},{33,1},{65,33},{97,65},{2,98}... | collective-permute-start | bytes 1368584 | tf_op jit(solution)/shard_map/ppermute | solution.py:60
  23.0 19.7 %collective-permute-start.1 = (bf16[96,2376]{1,0:T(8,128)(2,1)}, bf16[96,2376]{1,0:T(8,128)(2,1)S(1)}, u32[]{:S(2)}, u32[]{:S(2)}) collective-permute-start(bf16[96,2376]{1,0:T(8,128)(2,1)} %get-tuple-element.24), channel_id=1, source_target_pairs={{0,96},{32,0},{64,32},{96,64},{1,97},{33,1},{65,33},{97,65},{2,98}... | collective-permute-start | bytes 1368584 | tf_op jit(solution)/shard_map/ppermute | solution.py:61
  26.2 17.1 %collective-permute-start.2 = (bf16[96,2376]{1,0:T(8,128)(2,1)}, bf16[96,2376]{1,0:T(8,128)(2,1)S(1)}, u32[]{:S(2)}, u32[]{:S(2)}) collective-permute-start(bf16[96,2376]{1,0:T(8,128)(2,1)} %get-tuple-element.25), channel_id=1, source_target_pairs={{0,32},{32,64},{64,96},{96,0},{1,33},{33,65},{65,97},{97,1},{2,34}... | collective-permute-start | bytes 1368584 | tf_op jit(solution)/shard_map/ppermute | solution.py:61
  30.7 20.0 %collective-permute-start.5 = (bf16[96,2376]{1,0:T(8,128)(2,1)S(1)}, bf16[96,2376]{1,0:T(8,128)(2,1)}, u32[]{:S(2)}, u32[]{:S(2)}) collective-permute-start(bf16[96,2376]{1,0:T(8,128)(2,1)S(1)} %collective-permute-done.3), channel_id=1, source_target_pairs={{0,32},{32,64},{64,96},{96,0},{1,33},{33,65},{65,97},{97,1},{2,34}... | collective-permute-start | bytes 1368584 | tf_op jit(solution)/shard_map/ppermute | solution.py:62
  33.0 19.8 %collective-permute-start.4 = (bf16[96,2376]{1,0:T(8,128)(2,1)S(1)}, bf16[96,2376]{1,0:T(8,128)(2,1)}, u32[]{:S(2)}, u32[]{:S(2)}) collective-permute-start(bf16[96,2376]{1,0:T(8,128)(2,1)S(1)} %collective-permute-done), channel_id=1, source_target_pairs={{0,96},{32,0},{64,32},{96,64},{1,97},{33,1},{65,33},{97,65},{2,98}... | collective-permute-start | bytes 1368584 | tf_op jit(solution)/shard_map/ppermute | solution.py:62
  42.7 1.4 copy-start.7
  43.3 13.9 %copy-start.5 = (bf16[96,2376]{1,0:T(8,128)(2,1)}, bf16[96,2376]{1,0:T(8,128)(2,1)S(1)}, u32[]{:S(2)}) copy-start(bf16[96,2376]{1,0:T(8,128)(2,1)S(1)} %collective-permute-done.2) | copy-start | bytes 1368580
  54.1 22.1 %collective-permute-start.6 = (f32[96,2376]{1,0:T(8,128)S(1)}, f32[96,2376]{1,0:T(8,128)S(1)}, u32[]{:S(2)}, u32[]{:S(2)}) collective-permute-start(f32[96,2376]{1,0:T(8,128)S(1)} %fusion.12), channel_id=1, source_target_pairs={{0,128},{128,0},{1,129},{129,1},{2,130},{130,2},{3,131},{131,3},{4... | collective-permute-start | bytes 2737160 | tf_op jit(solution)/shard_map/ppermute | solution.py:93
  78.4 6.2 %copy-start.2 = (s32[768]{0:T(1024)S(1)}, s32[768]{0:T(1024)}, u32[]{:S(2)}) copy-start(s32[768]{0:T(1024)} %param.8) | copy-start | bytes 9220
  78.4 35.7 %all-to-all-start.1 = ((f32[3,32,2376]{2,1,0:T(8,128)}), f32[3,32,2376]{2,1,0:T(8,128)S(1)}, u32[]{:S(2)}, u32[]{:S(2)}) async-start(f32[3,32,2376]{2,1,0:T(8,128)} %bitcast.19), calls=%async_computation.1 | async-start | bytes 1867776 | tf_op jit(solution)/shard_map/all_to_all | solution.py:16
  115.8 6.3 %copy-start.1 = (s32[192]{0:T(256)S(1)}, s32[192]{0:T(256)}, u32[]{:S(2)}) copy-start(s32[192]{0:T(256)} %param.11) | copy-start | bytes 2308
  115.8 38.8 %all-to-all-start.2 = ((bf16[6,32,2432]{2,1,0:T(8,128)(2,1)}), bf16[6,32,2432]{2,1,0:T(8,128)(2,1)S(1)}, u32[]{:S(2)}, u32[]{:S(2)}) async-start(bf16[6,32,2432]{2,1,0:T(8,128)(2,1)} %broadcast_in_dim.55), calls=%async_computation.2 | async-start | bytes 1867776 | tf_op jit(solution)/shard_map/all_to_all | solution.py:16
  155.1 1.0 copy-start.8
  160.2 21.8 %collective-permute-start.7 = (f32[192,256]{1,0:T(8,128)}, f32[192,256]{1,0:T(8,128)S(1)}, u32[]{:S(2)}, u32[]{:S(2)}) collective-permute-start(f32[192,256]{1,0:T(8,128)} %concatenate.128), channel_id=1, source_target_pairs={{0,32},{32,64},{64,96},{96,0},{1,33},{33,65},{65,97},{97,1},{2,34}... | collective-permute-start | bytes 589832 | tf_op jit(solution)/shard_map/ppermute | solution.py:121
  169.4 5.1 %copy-start.6 = (bf16[96,2376]{1,0:T(8,128)(2,1)S(1)}, bf16[96,2376]{1,0:T(8,128)(2,1)}, u32[]{:S(2)}) copy-start(bf16[96,2376]{1,0:T(8,128)(2,1)} %copy-done.5) | copy-start | bytes 1368580
  169.4 12.6 %collective-permute-start.8 = (f32[192,256]{1,0:T(8,128)}, f32[192,256]{1,0:T(8,128)}, u32[]{:S(2)}, u32[]{:S(2)}) collective-permute-start(f32[192,256]{1,0:T(8,128)} %concatenate.129), channel_id=1, source_target_pairs={{0,64},{32,96},{64,0},{96,32},{1,65},{33,97},{65,1},{97,33},{2,66}... | collective-permute-start | bytes 589832 | tf_op jit(solution)/shard_map/ppermute | solution.py:121
  174.5 0.9 copy-start.9
  176.4 6.6 %collective-permute-start.9 = (f32[192,256]{1,0:T(8,128)}, f32[192,256]{1,0:T(8,128)S(1)}, u32[]{:S(2)}, u32[]{:S(2)}) collective-permute-start(f32[192,256]{1,0:T(8,128)} %concatenate.130), channel_id=1, source_target_pairs={{0,96},{32,0},{64,32},{96,64},{1,97},{33,1},{65,33},{97,65},{2,98}... | collective-permute-start | bytes 589832 | tf_op jit(solution)/shard_map/ppermute | solution.py:121
  186.7 10.1 %collective-permute-start.10 = (f32[416,256]{1,0:T(8,128)S(1)}, f32[416,256]{1,0:T(8,128)S(1)}, u32[]{:S(2)}, u32[]{:S(2)}) collective-permute-start(f32[416,256]{1,0:T(8,128)S(1)} %slice.308), channel_id=1, source_target_pairs={{0,1},{1,0},{2,3},{3,2},{4,5},{5,4},{6,7},{7,6},{8,9},{9,8},{10,11... | collective-permute-start | bytes 1277960 | tf_op jit(solution)/shard_map/ppermute | solution.py:133
  193.3 3.3 %collective-permute-start.11 = (bf16[384,192]{0,1:T(8,128)(2,1)S(1)}, bf16[384,192]{0,1:T(8,128)(2,1)S(1)}, u32[]{:S(2)}, u32[]{:S(2)}) collective-permute-start(bf16[384,192]{0,1:T(8,128)(2,1)S(1)} %slice.313), channel_id=1, source_target_pairs={{0,1},{1,0},{2,3},{3,2},{4,5},{5,4},{6,7},{7,6},{8,9},{9,8},{10,11... | collective-permute-start | bytes 442376 | tf_op jit(solution)/shard_map/ppermute | solution.py:82
  200.1 8.3 %copy-start.3 = (s32[192]{0:T(256)S(1)}, s32[192]{0:T(256)}, u32[]{:S(2)}) copy-start(s32[192]{0:T(256)} %param.10) | copy-start | bytes 2308
  200.1 31.2 %all-to-all-start.3 = ((f32[8,104,192]{1,2,0:T(8,128)}), f32[8,104,192]{1,2,0:T(8,128)S(1)}, u32[]{:S(2)}, u32[]{:S(2)}) async-start(f32[8,104,192]{1,2,0:T(8,128)} %copy.61), calls=%async_computation.3 | async-start | bytes 1572864 | tf_op jit(solution)/shard_map/all_to_all | solution.py:16
  233.1 11.4 %collective-permute-start.12 = (f32[56,192]{1,0:T(8,128)S(1)}, f32[56,192]{1,0:T(8,128)S(1)}, u32[]{:S(2)}, u32[]{:S(2)}) collective-permute-start(f32[56,192]{1,0:T(8,128)S(1)} %concatenate.142), channel_id=1, source_target_pairs={{0,2},{2,0},{1,3},{3,1},{4,6},{6,4},{5,7},{7,5},{8,10},{10,8},{9,1... | collective-permute-start | bytes 129032 | tf_op jit(solution)/shard_map/ppermute | solution.py:162
